TPU v7x, 512 devices: a whole 4x8x8 slice. The times are simulated.
512 devices in a mesh: seq: 128 (over z, x_hi, y), head: 4 (over x_lo, core).
Axes of the slice: x: 4 (x_hi: 2, x_lo: 2; x = x_hi * 2 + x_lo), y: 8, z: 8, core: 2. Of those that a mesh axis runs over, the one named last changes fastest.
Arguments:
- qkv: bfloat16 [2, 3, 16384, 8, 128], P(None, None, 'seq', 'head'), may hold values from -48 to 48
- out_weight: bfloat16 [2, 8, 128, 2048], P(None, 'head'), may hold values from -0.59765625 to 0.59765625
- out_grad: bfloat16 [16384, 2048], P('seq', 'head'), may hold values from -6 to 6
Outputs:
- mixed: bfloat16 [16384, 2048], P('seq', 'head')
- grads: bfloat16 [2, 3, 16384, 8, 128], P(None, None, 'seq', 'head')
All inputs are finite; a program needn't handle non-finite values.
Results may differ from a plain program's by a relative error of at most 0.039.
Values may be sent and summed in bfloat16 or wider, within the bound.
No kernel may reach another device: no remote copies, remote signals or barrier semaphores. Data moves between devices by JAX's collectives and lax.ppermute only.
A program may use at most 64 MiB of HBM per device.

v0:
```python
import functools
import math

import jax
import jax.numpy as jnp
from jax import lax
from jax.experimental import pallas as pl
from jax.experimental.pallas import tpu as pltpu
from jax.sharding import Mesh
from jax.sharding import PartitionSpec as P

ROW = 512
SCRATCH = 24 * 2**20
F32 = jnp.float32
BF16 = jnp.bfloat16


def dot(a, b, dims):
    return lax.dot_general(a, b, (dims, ((), ())), preferred_element_type=F32)


def mm(a, b):
    return dot(a, b, ((1,), (0,)))


def mm_nt(a, b):
    return dot(a, b, ((1,), (1,)))


def mm_tn(a, b):
    return dot(a, b, ((0,), (0,)))


def iota(shape, axis):
    return lax.broadcasted_iota(jnp.int32, shape, axis)


def attend(q, k, v, g, allowed, scale):
    scores = jnp.where(allowed, mm_nt(q, k) * scale, -jnp.inf)
    largest = jnp.max(scores, axis=1, keepdims=True)
    raised = jnp.exp(scores - largest)
    probs = raised * (1.0 / jnp.sum(raised, axis=1, keepdims=True))
    rounded = probs.astype(BF16)
    out = mm(rounded, v).astype(BF16)
    delta = jnp.sum(g.astype(F32) * out.astype(F32), axis=1, keepdims=True)
    gs = (probs * (mm_nt(g, v) - delta)).astype(BF16)
    return out, mm(gs, k) * scale, mm_tn(gs, q) * scale, mm_tn(rounded, g)


def rows_of(g, rows, heads, hd, tokens):
    total = 0
    for h in range(heads):
        pick = iota((rows, tokens), 0) == heads * iota((rows, tokens), 1) + h
        total = total + mm_nt(pick.astype(BF16), g[h * hd : (h + 1) * hd])
    return total


def grad_heads_kernel(heads, og_ref, w_ref, x_ref, send_ref, w_mem, x_mem, sems):
    lines, _, span, hd = send_ref.shape
    parts, tokens, width = og_ref.shape
    loads = [
        pltpu.make_async_copy(
            w_ref.at[heads * hd :, p * width : (p + 1) * width], w_mem.at[p], sems.at[p]
        )
        for p in range(parts)
    ]
    loads.append(pltpu.make_async_copy(x_ref.at[1], x_mem, sems.at[parts]))
    for load in loads:
        load.start()
    g = 0
    for p in range(parts):
        loads[p].wait()
        g = g + mm_nt(w_mem[p], og_ref[p])
    g = rows_of(g.astype(BF16), lines * span, heads, hd, tokens)
    send_ref[:, 3] = g.reshape(lines, span, hd).astype(BF16)
    loads[parts].wait()
    for kind in range(3):
        send_ref[:, kind] = x_mem[kind].astype(F32).reshape(lines, span, hd).astype(BF16)


def strided_kernel(scale, in_ref, out_ref):
    lines, _, span, hd = in_ref.shape
    rows = lines * span

    def part(kind):
        return in_ref[:, kind].astype(F32).reshape(rows, hd).astype(BF16)

    at, to = iota((rows, rows), 0), iota((rows, rows), 1)
    allowed = (at >= to) & (at % span == to % span)
    results = attend(part(0), part(1), part(2), part(3), allowed, scale)
    for kind, value in enumerate(results):
        out_ref[:, kind] = value.astype(F32).reshape(lines, span, hd).astype(BF16)


def by_token(value, heads):
    rows, _ = value.shape
    shape = (rows // heads, rows)
    picks = [iota(shape, 1) == heads * iota(shape, 0) + h for h in range(heads)]
    return jnp.concatenate([mm(p.astype(BF16), value).astype(BF16) for p in picks], axis=1)


def local_kernel(
    heads, scale, rank_ref, x_ref, og_ref, w_ref, a_ref, b_ref, c_ref,
    three_ref, four_ref, attended_ref, dq_ref, mid_ref, two_ref, one_ref,
    attended_mem, dq_mem, mid_mem, two_mem, one_mem, sems,
):
    rows, hd = dq_ref.shape
    tokens = rows // heads
    parts, _, width = og_ref.shape
    g = sum(
        mm_nt(w_ref[: heads * hd, p * width : (p + 1) * width], og_ref[p]) for p in range(parts)
    ).astype(BF16)
    same = (iota((tokens, tokens), 0) == iota((tokens, tokens), 1)).astype(BF16)

    at = iota((rows, 1), 0)
    apart = (iota((rows, rows), 1) == at % tokens * heads + at // tokens).astype(BF16)

    def split(first, second):
        return mm(apart, jnp.concatenate([first, second], axis=1)).astype(BF16)

    def joined(first, second):
        both = jnp.concatenate([first.astype(BF16), second.astype(BF16)], axis=1)
        both = mm_tn(apart, both).astype(BF16)
        return both[:, :hd], both[:, hd:]

    query = mm(apart, x_ref[0, 0]).astype(BF16)
    shards = [
        split(c_ref[0], c_ref[1]),
        split(b_ref[1, 0], b_ref[1, 1]),
        split(a_ref[0], a_ref[1]),
        split(b_ref[0, 0], b_ref[0, 1]),
        split(x_ref[0, 1], x_ref[0, 2]),
    ]
    back = ROW // tokens
    shape = (tokens, (back + 1) * tokens)
    to = iota(shape, 1)
    gap = iota((tokens, 1), 0) + back * tokens - to
    first = (back - rank_ref[0]) * tokens
    allowed = (gap >= 0) & (gap < ROW) & (to >= first)
    results = []
    for h in range(heads):
        mine = slice(h * tokens, (h + 1) * tokens)
        keys = jnp.concatenate([s[mine, :hd] for s in shards], axis=0)
        values = jnp.concatenate([s[mine, hd:] for s in shards], axis=0)
        own_g = mm_nt(same, g[h * hd : (h + 1) * hd]).astype(BF16)
        results.append(attend(query[mine], keys, values, own_g, allowed, scale))
    outs, dqs, dks, dvs = zip(*results)
    attended_mem[...] = jnp.concatenate(outs, axis=1)
    dq_mem[...] = mm_tn(apart, jnp.concatenate(dqs, axis=0).astype(BF16)).astype(BF16)
    blocks = []
    for j in range(back + 1):
        mine = slice(j * tokens, (j + 1) * tokens)
        blocks.append(
            joined(*(jnp.concatenate([v[mine] for v in each], axis=0) for each in (dks, dvs)))
        )
    four, three, two, one, mid = blocks
    for kind in range(2):
        mid_mem[kind] = mid[kind]
        two_mem[kind] = two[kind]
        one_mem[kind] = one[kind]
        three_ref[kind] = three[kind]
        four_ref[kind] = four[kind]
    pairs = (
        (attended_mem, attended_ref),
        (dq_mem, dq_ref),
        (mid_mem, mid_ref),
        (two_mem, two_ref),
        (one_mem, one_ref),
    )
    stores = [pltpu.make_async_copy(m, r, sems.at[n]) for n, (m, r) in enumerate(pairs)]
    for store in stores:
        store.start()
    for store in stores:
        store.wait()


def project_kernel(heads, attended_ref, back_ref, w_ref, out_ref, attended_mem, sem):
    load = pltpu.make_async_copy(attended_ref, attended_mem, sem.at[0])
    load.start()
    lines, _, span, hd = back_ref.shape
    parts, _, width = out_ref.shape
    strided = by_token(back_ref[:, 0].astype(F32).reshape(lines * span, hd).astype(BF16), heads)
    load.wait()
    attended = jnp.concatenate([attended_mem[...], strided], axis=1)
    for p in range(parts):
        out_ref[p] = mm(attended, w_ref[:, p * width : (p + 1) * width]).astype(BF16)


def finish_kernel(sums_ref, dq_ref, mid_ref, *refs):
    *returns, back_ref, mixed_ref, grads_ref = refs
    mixed_ref[...] = sum(sums_ref[p].astype(F32) for p in range(sums_ref.shape[0])).astype(BF16)
    rows, hd = dq_ref.shape
    grads_ref[0, 0] = dq_ref[...]
    for kind in range(2):
        total = mid_ref[kind].astype(F32) + sum(r[kind].astype(F32) for r in returns)
        grads_ref[0, 1 + kind] = total.astype(BF16)
    for kind in range(3):
        grads_ref[1, kind] = back_ref[:, 1 + kind].astype(F32).reshape(rows, hd).astype(BF16)


def call(kernel, outs, *args, far=(), away=(), scratch=()):
    vmem, smem, hbm = [pl.BlockSpec(memory_space=m) for m in (pltpu.VMEM, pltpu.SMEM, pltpu.HBM)]
    ins = [smem if a.dtype == jnp.int32 else hbm if n in far else vmem for n, a in enumerate(args)]
    args = [
        pltpu.with_memory_space_constraint(a, pltpu.HBM) if n in far else a
        for n, a in enumerate(args)
    ]
    made = [(pltpu.HBM if n in away else jax.ShapeDtypeStruct)(*o) for n, o in enumerate(outs)]
    return pl.pallas_call(
        kernel,
        out_shape=made,
        in_specs=ins,
        out_specs=[hbm if n in away else vmem for n in range(len(outs))],
        scratch_shapes=[
            pltpu.VMEM(*s) if isinstance(s, tuple) else pltpu.SemaphoreType.DMA((s,)) for s in scratch
        ],
        compiler_params=pltpu.CompilerParams(vmem_limit_bytes=SCRATCH),
    )(*args)


def layer(qkv, out_weight, out_grad):
    _, _, tokens, heads, hd = qkv.shape
    lines = lax.axis_size("line")
    quarters = lax.axis_size("quarter")
    parts = lax.axis_size("head")
    seq = ("line", "quarter")
    count = lines * quarters
    rank = (lax.axis_index("line") * quarters + lax.axis_index("quarter")).astype(jnp.int32)
    scale = 1.0 / math.sqrt(hd)
    rows = tokens * heads
    span = rows // lines
    width = out_grad.shape[1]
    kernel = functools.partial

    def shifted(value, steps):
        pairs = [(i, i + steps) for i in range(count) if 0 <= i + steps < count]
        return lax.ppermute(value, seq, pairs)

    x = qkv.reshape(2, 3, rows, hd)
    w = out_weight.reshape(2 * heads * hd, parts * width)

    pair = x[0, 1:3]
    a = shifted(pair, 2)
    og = lax.all_gather(out_grad, "head", axis=0)
    both = jnp.stack([lax.optimization_barrier((x, a))[0][0, 1:3], a])
    b = shifted(both, 1)
    c = shifted(a, 2)
    (send,) = call(
        kernel(grad_heads_kernel, heads),
        [((lines, 4, span, hd), BF16)],
        og,
        w,
        x,
        far=(1, 2),
        scratch=(((parts, heads * hd, width), BF16), ((3, rows, hd), BF16), parts + 1),
    )
    got = lax.all_to_all(send, "line", 0, 0, tiled=True)
    flat, pair_of = (rows, hd), (2, rows, hd)
    flat, pair_of, wide = (rows, hd), (2, rows, hd), (tokens, heads * hd)
    away = (wide, flat, pair_of, pair_of, pair_of)
    three, four, attended, local_dq, mid, two, one = call(
        kernel(local_kernel, heads, scale),
        [(o, BF16) for o in (pair_of, pair_of, *away)],
        rank.reshape(1),
        x,
        og,
        w,
        a,
        b,
        c,
        away=(2, 3, 4, 5, 6),
        scratch=(*((o, BF16) for o in away), len(away)),
    )
    returns = [shifted(v, -n) for n, v in ((1, one), (2, two), (3, three), (4, four))]
    (results,) = call(kernel(strided_kernel, scale), [(got.shape, BF16)], got)
    returned = lax.all_to_all(results, "line", 0, 0, tiled=True)
    (partial,) = call(
        kernel(project_kernel, heads),
        [((parts, tokens, width), BF16)],
        attended,
        returned,
        w,
        far=(0,),
        scratch=((wide, BF16), 1),
    )
    sums = lax.all_to_all(partial, "head", 0, 0, tiled=True)
    mixed, grads = call(
        finish_kernel,
        [((tokens, width), BF16), ((2, 3, rows, hd), BF16)],
        sums,
        local_dq,
        mid,
        *returns,
        returned,
    )
    return mixed, grads.reshape(qkv.shape)


def solution(mesh):
    count = mesh.shape["seq"]
    split = Mesh(
        mesh.devices.reshape(count // 4, 4, mesh.shape["head"]), ("line", "quarter", "head")
    )
    seq = ("line", "quarter")
    return jax.shard_map(
        layer,
        mesh=split,
        in_specs=(
            P(None, None, seq, "head", None),
            P(None, "head", None, None),
            P(seq, "head"),
        ),
        out_specs=(P(seq, "head"), P(None, None, seq, "head", None)),
        check_vma=False,
    )
```

profile of v0, /device:TPU:62, one launch (start us, length us, event | category | flops | bytes accessed | tf_op | source)
XLA Modules:
  0.0 118.2 jit_solution(12105693795981791675)
XLA Ops:
  0.6 0.0 copy-start.1
  0.6 7.1 %all-gather = bf16[512,512]{1,0:T(8,128)(2,1)S(1)} all-gather(bf16[128,512]{1,0:T(8,128)(2,1)} %param.5), channel_id=2, replica_groups=mesh['line'=32,'quarter'=4,'head'=4] {'head'}, dimensions={0}, use_global_device_ids=true | all-gather | bytes 655360 | tf_op jit(solution)/shard_map/all_gather | solution.py:244
  7.8 2.8 %shard_map.51 = bf16[32,4,8,128]{3,2,1,0:T(8,128)(2,1)} custom-call(bf16[4,128,512]{2,1,0:T(8,128)(2,1)S(1)} %bitcast.11, bf16[512,2048]{1,0:T(8,128)(2,1)} %bitcast.8, bf16[2,3,256,128]{3,2,1,0:T(8,128)(2,1)} %bitcast.13), custom_call_target="tpu_custom_call" | custom-call | tf_op jit(solution)/shard_map/pallas_call | solution.py:209
  10.6 0.0 copy-start
  10.6 18.4 %all-to-all-start = ((bf16[32,4,8,128]{3,2,1,0:T(8,128)(2,1)}), bf16[32,4,8,128]{3,2,1,0:T(8,128)(2,1)S(1)}, u32[]{:S(2)}, u32[]{:S(2)}) async-start(bf16[32,4,8,128]{3,2,1,0:T(8,128)(2,1)} %shard_map.51), calls=%async_computation | async-start | bytes 524288 | tf_op jit(solution)/shard_map/all_to_all | solution.py:257
  29.0 0.0 copy-done.1
  29.0 3.1 %collective-permute-start = (bf16[2,256,128]{2,1,0:T(8,128)(2,1)S(1)}, bf16[2,256,128]{2,1,0:T(8,128)(2,1)S(1)}, u32[]{:S(2)}, u32[]{:S(2)}) collective-permute-start(bf16[2,256,128]{2,1,0:T(8,128)(2,1)S(1)} %slice_bitcast_fusion), channel_id=1, source_target_pairs={{0,8},{4,12},{8,16},{12,20},{16,24},{20,28},{24,32},{28,36},{32,40... | collective-permute-start | bytes 393224 | tf_op jit(solution)/shard_map/ppermute | solution.py:237
  32.2 8.6 %all-to-all-done.in_ref = bf16[32,4,8,128]{3,2,1,0:T(8,128)(2,1)S(1)} async-done(((bf16[32,4,8,128]{3,2,1,0:T(8,128)(2,1)}), bf16[32,4,8,128]{3,2,1,0:T(8,128)(2,1)S(1)}, u32[]{:S(2)}, u32[]{:S(2)}) %all-to-all-start) | async-done | bytes 262176 | tf_op jit(solution)/shard_map/all_to_all | solution.py:257
  40.7 1.6 %shard_map.52 = bf16[32,4,8,128]{3,2,1,0:T(8,128)(2,1)} custom-call(bf16[32,4,8,128]{3,2,1,0:T(8,128)(2,1)S(1)} %all-to-all-done.in_ref), custom_call_target="tpu_custom_call" | custom-call | tf_op jit(solution)/shard_map/pallas_call | solution.py:209
  42.3 9.8 %all-to-all-start.1 = ((bf16[32,4,8,128]{3,2,1,0:T(8,128)(2,1)}), bf16[32,4,8,128]{3,2,1,0:T(8,128)(2,1)S(1)}, u32[]{:S(2)}, u32[]{:S(2)}) async-start(bf16[32,4,8,128]{3,2,1,0:T(8,128)(2,1)} %shard_map.52), calls=%async_computation.1 | async-start | bytes 524288 | tf_op jit(solution)/shard_map/all_to_all | solution.py:276
  52.1 0.0 collective-permute-done.a_ref
  52.1 0.7 pad_maximum_fusion
  52.9 3.3 %collective-permute-start.1 = (bf16[2,2,256,128]{3,2,1,0:T(8,128)(2,1)}, bf16[2,2,256,128]{3,2,1,0:T(8,128)(2,1)}, u32[]{:S(2)}, u32[]{:S(2)}) collective-permute-start(bf16[2,2,256,128]{3,2,1,0:T(8,128)(2,1)} %pad_maximum_fusion), channel_id=1, source_target_pairs={{0,4},{4,8},{8,12},{12,16},{16,20},{20,24},{24,28},{28,32},{32,36}... | collective-permute-start | bytes 786440 | tf_op jit(solution)/shard_map/ppermute | solution.py:237
  56.2 5.4 %collective-permute-start.2 = (bf16[2,256,128]{2,1,0:T(8,128)(2,1)S(1)}, bf16[2,256,128]{2,1,0:T(8,128)(2,1)S(1)}, u32[]{:S(2)}, u32[]{:S(2)}) collective-permute-start(bf16[2,256,128]{2,1,0:T(8,128)(2,1)S(1)} %collective-permute-done.a_ref), channel_id=1, source_target_pairs={{0,8},{4,12},{8,16},{12,20},{16,24},{20,28},{24,32},{28,36},{32,40... | collective-permute-start | bytes 393224 | tf_op jit(solution)/shard_map/ppermute | solution.py:237
  61.6 9.7 %collective-permute-done.2.c_ref = bf16[2,256,128]{2,1,0:T(8,128)(2,1)S(1)} collective-permute-done((bf16[2,256,128]{2,1,0:T(8,128)(2,1)S(1)}, bf16[2,256,128]{2,1,0:T(8,128)(2,1)S(1)}, u32[]{:S(2)}, u32[]{:S(2)}) %collective-permute-start.2) | collective-permute-done | bytes 131104 | tf_op jit(solution)/shard_map/ppermute | solution.py:237
  71.3 0.0 collective-permute-done.1.b_ref
  71.3 0.0 copy-done
  71.3 4.4 %shard_map.50 = (bf16[2,256,128]{2,1,0:T(8,128)(2,1)S(1)}, bf16[2,256,128]{2,1,0:T(8,128)(2,1)S(1)}, bf16[128,256]{1,0:T(8,128)(2,1)}, bf16[256,128]{1,0:T(8,128...) custom-call(s32[1]{0:T(128)} %bitcast.rank_ref, ...), custom_call_target="tpu_custom_call" | custom-call | tf_op jit(solution)/shard_map/pallas_call | solution.py:209
  75.7 0.0 copy-start.4
  75.7 0.6 copy-done.4
  76.3 0.0 copy-start.6
  76.3 0.7 copy-done.6
  77.0 0.0 copy-start.8
  77.0 0.0 copy-start.2
  77.0 0.0 copy-start.3
  77.0 0.0 all-to-all-done.1.back_ref.refs_4_
  77.0 0.0 copy-start.7
  77.0 0.0 copy-start.5
  77.0 2.2 %shard_map.53 = bf16[4,128,512]{2,1,0:T(8,128)(2,1)} custom-call(bf16[128,256]{1,0:T(8,128)(2,1)} %get-tuple-element.13.attended_ref, bf16[32,4,8,128]{3,2,1,0:T(8,128)(2,1)S(1)} %all-to-all-done.1.back_ref.refs_4_, bf16[512,2048]{1,0:T(8,128)(2,1)S(1)} %bitcast.10), custom_call_target="tpu_custom_call" | custom-call | tf_op jit(solution)/shard_map/pallas_call | solution.py:209
  79.2 4.4 %all-to-all-start.2 = ((bf16[4,128,512]{2,1,0:T(8,128)(2,1)}), bf16[4,128,512]{2,1,0:T(8,128)(2,1)S(1)}, u32[]{:S(2)}, u32[]{:S(2)}) async-start(bf16[4,128,512]{2,1,0:T(8,128)(2,1)} %shard_map.53), calls=%async_computation.2 | async-start | bytes 1048576 | tf_op jit(solution)/shard_map/all_to_all | solution.py:286
  83.6 1.9 %collective-permute-start.3 = (bf16[2,256,128]{2,1,0:T(8,128)(2,1)}, bf16[2,256,128]{2,1,0:T(8,128)(2,1)S(1)}, u32[]{:S(2)}, u32[]{:S(2)}) collective-permute-start(bf16[2,256,128]{2,1,0:T(8,128)(2,1)} %get-tuple-element.16), channel_id=1, source_target_pairs={{4,0},{8,4},{12,8},{16,12},{20,16},{24,20},{28,24},{32,28},{36,32}... | collective-permute-start | bytes 393224 | tf_op jit(solution)/shard_map/ppermute | solution.py:237
  85.5 0.0 copy-done.8
  85.5 3.3 %collective-permute-start.4 = (bf16[2,256,128]{2,1,0:T(8,128)(2,1)S(1)}, bf16[2,256,128]{2,1,0:T(8,128)(2,1)S(1)}, u32[]{:S(2)}, u32[]{:S(2)}) collective-permute-start(bf16[2,256,128]{2,1,0:T(8,128)(2,1)S(1)} %copy-done.8), channel_id=1, source_target_pairs={{8,0},{12,4},{16,8},{20,12},{24,16},{28,20},{32,24},{36,28},{40,32... | collective-permute-start | bytes 393224 | tf_op jit(solution)/shard_map/ppermute | solution.py:237
  88.8 0.0 copy-done.7
  88.9 6.9 %collective-permute-start.5 = (bf16[2,256,128]{2,1,0:T(8,128)(2,1)S(1)}, bf16[2,256,128]{2,1,0:T(8,128)(2,1)S(1)}, u32[]{:S(2)}, u32[]{:S(2)}) collective-permute-start(bf16[2,256,128]{2,1,0:T(8,128)(2,1)S(1)} %copy-done.7), channel_id=1, source_target_pairs={{12,0},{16,4},{20,8},{24,12},{28,16},{32,20},{36,24},{40,28},{44,3... | collective-permute-start | bytes 393224 | tf_op jit(solution)/shard_map/ppermute | solution.py:237
  95.8 0.0 copy-done.5
  95.8 3.8 %collective-permute-start.6 = (bf16[2,256,128]{2,1,0:T(8,128)(2,1)S(1)}, bf16[2,256,128]{2,1,0:T(8,128)(2,1)S(1)}, u32[]{:S(2)}, u32[]{:S(2)}) collective-permute-start(bf16[2,256,128]{2,1,0:T(8,128)(2,1)S(1)} %copy-done.5), channel_id=1, source_target_pairs={{16,0},{20,4},{24,8},{28,12},{32,16},{36,20},{40,24},{44,28},{48,3... | collective-permute-start | bytes 393224 | tf_op jit(solution)/shard_map/ppermute | solution.py:237
  99.5 0.0 collective-permute-done.3.refs_0_
  99.5 0.9 collective-permute-done.4.refs_1_
  100.5 16.9 %collective-permute-done.5.refs_2_ = bf16[2,256,128]{2,1,0:T(8,128)(2,1)S(1)} collective-permute-done((bf16[2,256,128]{2,1,0:T(8,128)(2,1)S(1)}, bf16[2,256,128]{2,1,0:T(8,128)(2,1)S(1)}, u32[]{:S(2)}, u32[]{:S(2)}) %collective-permute-start.5) | collective-permute-done | bytes 131104 | tf_op jit(solution)/shard_map/ppermute | solution.py:237
  117.3 0.0 collective-permute-done.6.refs_3_
  117.3 0.0 all-to-all-done.2.sums_ref
  117.3 0.0 copy-done.2
  117.3 0.0 copy-done.3
  117.3 0.9 shard_map.54
  (2 shorter events, 0.0 us)
Async XLA Ops:
  0.6 28.4 %copy-start.1 = (bf16[2,3,128,2,128]{4,3,2,1,0:T(2,128)(2,1)S(1)}, bf16[2,3,128,2,128]{4,3,2,1,0:T(2,128)(2,1)}, u32[]{:S(2)}) copy-start(bf16[2,3,128,2,128]{4,3,2,1,0:T(2,128)(2,1)} %param.3) | copy-start | bytes 1179652
  10.6 60.7 %copy-start = (bf16[2,2,128,2048]{3,2,1,0:T(8,128)(2,1)S(1)}, bf16[2,2,128,2048]{3,2,1,0:T(8,128)(2,1)}, u32[]{:S(2)}) copy-start(bf16[2,2,128,2048]{3,2,1,0:T(8,128)(2,1)} %param.4) | copy-start | bytes 6291460
  10.6 30.1 %all-to-all-start = ((bf16[32,4,8,128]{3,2,1,0:T(8,128)(2,1)}), bf16[32,4,8,128]{3,2,1,0:T(8,128)(2,1)S(1)}, u32[]{:S(2)}, u32[]{:S(2)}) async-start(bf16[32,4,8,128]{3,2,1,0:T(8,128)(2,1)} %shard_map.51), calls=%async_computation | async-start | bytes 524288 | tf_op jit(solution)/shard_map/all_to_all | solution.py:257
  29.0 23.1 %collective-permute-start = (bf16[2,256,128]{2,1,0:T(8,128)(2,1)S(1)}, bf16[2,256,128]{2,1,0:T(8,128)(2,1)S(1)}, u32[]{:S(2)}, u32[]{:S(2)}) collective-permute-start(bf16[2,256,128]{2,1,0:T(8,128)(2,1)S(1)} %slice_bitcast_fusion), channel_id=1, source_target_pairs={{0,8},{4,12},{8,16},{12,20},{16,24},{20,28},{24,32},{28,36},{32,40... | collective-permute-start | bytes 393224 | tf_op jit(solution)/shard_map/ppermute | solution.py:237
  42.3 34.6 %all-to-all-start.1 = ((bf16[32,4,8,128]{3,2,1,0:T(8,128)(2,1)}), bf16[32,4,8,128]{3,2,1,0:T(8,128)(2,1)S(1)}, u32[]{:S(2)}, u32[]{:S(2)}) async-start(bf16[32,4,8,128]{3,2,1,0:T(8,128)(2,1)} %shard_map.52), calls=%async_computation.1 | async-start | bytes 524288 | tf_op jit(solution)/shard_map/all_to_all | solution.py:276
  52.9 18.4 %collective-permute-start.1 = (bf16[2,2,256,128]{3,2,1,0:T(8,128)(2,1)}, bf16[2,2,256,128]{3,2,1,0:T(8,128)(2,1)}, u32[]{:S(2)}, u32[]{:S(2)}) collective-permute-start(bf16[2,2,256,128]{3,2,1,0:T(8,128)(2,1)} %pad_maximum_fusion), channel_id=1, source_target_pairs={{0,4},{4,8},{8,12},{12,16},{16,20},{20,24},{24,28},{28,32},{32,36}... | collective-permute-start | bytes 786440 | tf_op jit(solution)/shard_map/ppermute | solution.py:237
  56.2 15.1 %collective-permute-start.2 = (bf16[2,256,128]{2,1,0:T(8,128)(2,1)S(1)}, bf16[2,256,128]{2,1,0:T(8,128)(2,1)S(1)}, u32[]{:S(2)}, u32[]{:S(2)}) collective-permute-start(bf16[2,256,128]{2,1,0:T(8,128)(2,1)S(1)} %collective-permute-done.a_ref), channel_id=1, source_target_pairs={{0,8},{4,12},{8,16},{12,20},{16,24},{20,28},{24,32},{28,36},{32,40... | collective-permute-start | bytes 393224 | tf_op jit(solution)/shard_map/ppermute | solution.py:237
  75.7 0.6 copy-start.4
  76.3 0.7 copy-start.6
  77.0 8.5 %copy-start.8 = (bf16[2,256,128]{2,1,0:T(8,128)(2,1)S(1)}, bf16[2,256,128]{2,1,0:T(8,128)(2,1)}, u32[]{:S(2)}) copy-start(bf16[2,256,128]{2,1,0:T(8,128)(2,1)} %get-tuple-element.17) | copy-start | bytes 393220
  77.0 40.4 %copy-start.2 = (bf16[2,256,128]{2,1,0:T(8,128)(2,1)S(1)}, bf16[2,256,128]{2,1,0:T(8,128)(2,1)}, u32[]{:S(2)}) copy-start(bf16[2,256,128]{2,1,0:T(8,128)(2,1)} %get-tuple-element.15.mid_ref) | copy-start | bytes 393220
  77.0 40.4 %copy-start.3 = (bf16[256,128]{1,0:T(8,128)(2,1)S(1)}, bf16[256,128]{1,0:T(8,128)(2,1)}, u32[]{:S(2)}) copy-start(bf16[256,128]{1,0:T(8,128)(2,1)} %get-tuple-element.14.dq_ref) | copy-start | bytes 196612
  77.0 11.9 %copy-start.7 = (bf16[2,256,128]{2,1,0:T(8,128)(2,1)S(1)}, bf16[2,256,128]{2,1,0:T(8,128)(2,1)}, u32[]{:S(2)}) copy-start(bf16[2,256,128]{2,1,0:T(8,128)(2,1)} %copy-done.6) | copy-start | bytes 393220
  77.0 18.8 %copy-start.5 = (bf16[2,256,128]{2,1,0:T(8,128)(2,1)S(1)}, bf16[2,256,128]{2,1,0:T(8,128)(2,1)}, u32[]{:S(2)}) copy-start(bf16[2,256,128]{2,1,0:T(8,128)(2,1)} %copy-done.4) | copy-start | bytes 393220
  79.2 38.1 %all-to-all-start.2 = ((bf16[4,128,512]{2,1,0:T(8,128)(2,1)}), bf16[4,128,512]{2,1,0:T(8,128)(2,1)S(1)}, u32[]{:S(2)}, u32[]{:S(2)}) async-start(bf16[4,128,512]{2,1,0:T(8,128)(2,1)} %shard_map.53), calls=%async_computation.2 | async-start | bytes 1048576 | tf_op jit(solution)/shard_map/all_to_all | solution.py:286
  83.6 16.0 %collective-permute-start.3 = (bf16[2,256,128]{2,1,0:T(8,128)(2,1)}, bf16[2,256,128]{2,1,0:T(8,128)(2,1)S(1)}, u32[]{:S(2)}, u32[]{:S(2)}) collective-permute-start(bf16[2,256,128]{2,1,0:T(8,128)(2,1)} %get-tuple-element.16), channel_id=1, source_target_pairs={{4,0},{8,4},{12,8},{16,12},{20,16},{24,20},{28,24},{32,28},{36,32}... | collective-permute-start | bytes 393224 | tf_op jit(solution)/shard_map/ppermute | solution.py:237
  85.5 15.0 %collective-permute-start.4 = (bf16[2,256,128]{2,1,0:T(8,128)(2,1)S(1)}, bf16[2,256,128]{2,1,0:T(8,128)(2,1)S(1)}, u32[]{:S(2)}, u32[]{:S(2)}) collective-permute-start(bf16[2,256,128]{2,1,0:T(8,128)(2,1)S(1)} %copy-done.8), channel_id=1, source_target_pairs={{8,0},{12,4},{16,8},{20,12},{24,16},{28,20},{32,24},{36,28},{40,32... | collective-permute-start | bytes 393224 | tf_op jit(solution)/shard_map/ppermute | solution.py:237
  88.9 28.5 %collective-permute-start.5 = (bf16[2,256,128]{2,1,0:T(8,128)(2,1)S(1)}, bf16[2,256,128]{2,1,0:T(8,128)(2,1)S(1)}, u32[]{:S(2)}, u32[]{:S(2)}) collective-permute-start(bf16[2,256,128]{2,1,0:T(8,128)(2,1)S(1)} %copy-done.7), channel_id=1, source_target_pairs={{12,0},{16,4},{20,8},{24,12},{28,16},{32,20},{36,24},{40,28},{44,3... | collective-permute-start | bytes 393224 | tf_op jit(solution)/shard_map/ppermute | solution.py:237
  95.8 21.5 %collective-permute-start.6 = (bf16[2,256,128]{2,1,0:T(8,128)(2,1)S(1)}, bf16[2,256,128]{2,1,0:T(8,128)(2,1)S(1)}, u32[]{:S(2)}, u32[]{:S(2)}) collective-permute-start(bf16[2,256,128]{2,1,0:T(8,128)(2,1)S(1)} %copy-done.5), channel_id=1, source_target_pairs={{16,0},{20,4},{24,8},{28,12},{32,16},{36,20},{40,24},{44,28},{48,3... | collective-permute-start | bytes 393224 | tf_op jit(solution)/shard_map/ppermute | solution.py:237
where the time goes:
time: 119 us; the launch traced here: 118 us
  starting transfers between devices  60.3 us (51%)
  waiting for transfers between devices  36 us (30%)
  Pallas kernels  11.9 us (10%)
  blocking collectives  7.11 us (6%)
  local copies, waits for them, and re-layouts  1.34 us (1%)
    ppermute x7, starting transfers between devices, shifted(): return lax.ppermute(value, seq, pairs)  27.8 us
    ppermute x7, waiting for transfers between devices, shifted(): return lax.ppermute(value, seq, pairs)  27.4 us
    all_to_all x1, starting transfers between devices, layer(): got = lax.all_to_all(send, 'line', 0, 0, tiled=True)  18.4 us
    pallas_call x5, Pallas kernels, call(): pl.pallas_call(kernel, out_shape=made, in_specs=ins, out_specs=[hbm if n...  11.9 us
    all_to_all x1, starting transfers between devices, layer(): returned = lax.all_to_all(results, 'line', 0, 0, tiled=True)  9.79 us
    all_to_all x1, waiting for transfers between devices, layer(): got = lax.all_to_all(send, 'line', 0, 0, tiled=True)  8.55 us
    all_gather x1, blocking collectives, layer(): og = lax.all_gather(out_grad, 'head', axis=0)  7.11 us
    all_to_all x1, starting transfers between devices, layer(): sums = lax.all_to_all(partial, 'head', 0, 0, tiled=True)  4.39 us
  transfers between devices with their start and end apart: 10, of which 4 were waited for; matrix products, arithmetic and copies ran while one was open for 1% of the time, Pallas kernels for 5%

commit v1 on v0

--- a/solution.py
+++ b/solution.py
@@ -67,15 +67,15 @@
     loads.append(pltpu.make_async_copy(x_ref.at[1], x_mem, sems.at[parts]))
     for load in loads:
         load.start()
+    loads[parts].wait()
+    for kind in range(3):
+        send_ref[:, kind] = x_mem[kind].astype(F32).reshape(lines, span, hd).astype(BF16)
     g = 0
     for p in range(parts):
         loads[p].wait()
         g = g + mm_nt(w_mem[p], og_ref[p])
     g = rows_of(g.astype(BF16), lines * span, heads, hd, tokens)
     send_ref[:, 3] = g.reshape(lines, span, hd).astype(BF16)
-    loads[parts].wait()
-    for kind in range(3):
-        send_ref[:, kind] = x_mem[kind].astype(F32).reshape(lines, span, hd).astype(BF16)
 
 
 def strided_kernel(scale, in_ref, out_ref):
@@ -99,73 +99,83 @@
     return jnp.concatenate([mm(p.astype(BF16), value).astype(BF16) for p in picks], axis=1)
 
 
-def local_kernel(
-    heads, scale, rank_ref, x_ref, og_ref, w_ref, a_ref, b_ref, c_ref,
-    three_ref, four_ref, attended_ref, dq_ref, mid_ref, two_ref, one_ref,
-    attended_mem, dq_mem, mid_mem, two_mem, one_mem, sems,
-):
-    rows, hd = dq_ref.shape
+def places(rows, heads):
     tokens = rows // heads
-    parts, _, width = og_ref.shape
+    at = iota((rows, 1), 0)
+    return (iota((rows, rows), 1) == at % tokens * heads + at // tokens).astype(BF16)
+
+
+def split_kernel(heads, x_ref, pair_ref, query_ref, x_mem, sem):
+    load = pltpu.make_async_copy(x_ref.at[0], x_mem, sem.at[0])
+    load.start()
+    rows, hd = query_ref.shape
+    apart = places(rows, heads)
+    load.wait()
+    whole = mm(apart, jnp.concatenate([x_mem[k] for k in range(3)], axis=1)).astype(BF16)
+    query_ref[...] = whole[:, :hd]
+    pair_ref[0] = whole[:, hd : 2 * hd]
+    pair_ref[1] = whole[:, 2 * hd :]
+
+
+def local_grad_kernel(heads, og_ref, w_ref, g_ref):
+    parts, tokens, width = og_ref.shape
+    hd = g_ref.shape[1]
     g = sum(
         mm_nt(w_ref[: heads * hd, p * width : (p + 1) * width], og_ref[p]) for p in range(parts)
     ).astype(BF16)
     same = (iota((tokens, tokens), 0) == iota((tokens, tokens), 1)).astype(BF16)
-
-    at = iota((rows, 1), 0)
-    apart = (iota((rows, rows), 1) == at % tokens * heads + at // tokens).astype(BF16)
-
-    def split(first, second):
-        return mm(apart, jnp.concatenate([first, second], axis=1)).astype(BF16)
-
-    def joined(first, second):
-        both = jnp.concatenate([first.astype(BF16), second.astype(BF16)], axis=1)
-        both = mm_tn(apart, both).astype(BF16)
-        return both[:, :hd], both[:, hd:]
-
-    query = mm(apart, x_ref[0, 0]).astype(BF16)
-    shards = [
-        split(c_ref[0], c_ref[1]),
-        split(b_ref[1, 0], b_ref[1, 1]),
-        split(a_ref[0], a_ref[1]),
-        split(b_ref[0, 0], b_ref[0, 1]),
-        split(x_ref[0, 1], x_ref[0, 2]),
-    ]
+    for h in range(heads):
+        own = mm_nt(same, g[h * hd : (h + 1) * hd])
+        g_ref[h * tokens : (h + 1) * tokens] = own.astype(BF16)
+
+
+def local_kernel(
+    heads, scale, rank_ref, query_ref, pair_ref, g_ref, a_ref, b_ref, c_ref,
+    one_three_ref, four_ref, attended_ref, dq_ref, mid_ref, two_ref,
+    attended_mem, dq_mem, mid_mem, two_mem, sems,
+):
+    rows, _ = dq_ref.shape
+    tokens = rows // heads
     back = ROW // tokens
     shape = (tokens, (back + 1) * tokens)
     to = iota(shape, 1)
     gap = iota((tokens, 1), 0) + back * tokens - to
     first = (back - rank_ref[0]) * tokens
     allowed = (gap >= 0) & (gap < ROW) & (to >= first)
-    results = []
+    outs = []
     for h in range(heads):
         mine = slice(h * tokens, (h + 1) * tokens)
-        keys = jnp.concatenate([s[mine, :hd] for s in shards], axis=0)
-        values = jnp.concatenate([s[mine, hd:] for s in shards], axis=0)
-        own_g = mm_nt(same, g[h * hd : (h + 1) * hd]).astype(BF16)
-        results.append(attend(query[mine], keys, values, own_g, allowed, scale))
-    outs, dqs, dks, dvs = zip(*results)
+
+        def window(kind):
+            return jnp.concatenate(
+                [
+                    c_ref[kind, mine],
+                    b_ref[1, kind, mine],
+                    a_ref[kind, mine],
+                    b_ref[0, kind, mine],
+                    pair_ref[kind, mine],
+                ],
+                axis=0,
+            )
+
+        out, dq, *pair = attend(query_ref[mine], window(0), window(1), g_ref[mine], allowed, scale)
+        outs.append(out)
+        dq_mem[mine] = dq.astype(BF16)
+        for kind, value in enumerate(pair):
+            four, three, two, one, mid = [
+                value[j * tokens : (j + 1) * tokens].astype(BF16) for j in range(back + 1)
+            ]
+            mid_mem[kind, mine] = mid
+            two_mem[kind, mine] = two
+            one_three_ref[0, kind, mine] = one
+            one_three_ref[1, kind, mine] = three
+            four_ref[kind, mine] = four
     attended_mem[...] = jnp.concatenate(outs, axis=1)
-    dq_mem[...] = mm_tn(apart, jnp.concatenate(dqs, axis=0).astype(BF16)).astype(BF16)
-    blocks = []
-    for j in range(back + 1):
-        mine = slice(j * tokens, (j + 1) * tokens)
-        blocks.append(
-            joined(*(jnp.concatenate([v[mine] for v in each], axis=0) for each in (dks, dvs)))
-        )
-    four, three, two, one, mid = blocks
-    for kind in range(2):
-        mid_mem[kind] = mid[kind]
-        two_mem[kind] = two[kind]
-        one_mem[kind] = one[kind]
-        three_ref[kind] = three[kind]
-        four_ref[kind] = four[kind]
     pairs = (
         (attended_mem, attended_ref),
         (dq_mem, dq_ref),
         (mid_mem, mid_ref),
         (two_mem, two_ref),
-        (one_mem, one_ref),
     )
     stores = [pltpu.make_async_copy(m, r, sems.at[n]) for n, (m, r) in enumerate(pairs)]
     for store in stores:
@@ -174,27 +184,40 @@
         store.wait()
 
 
+def combine_kernel(two_ref, d_ref, out_ref, two_mem, sem):
+    load = pltpu.make_async_copy(two_ref, two_mem, sem.at[0])
+    load.start()
+    load.wait()
+    out_ref[...] = (two_mem[...].astype(F32) + d_ref[1].astype(F32)).astype(BF16)
+
+
 def project_kernel(heads, attended_ref, back_ref, w_ref, out_ref, attended_mem, sem):
     load = pltpu.make_async_copy(attended_ref, attended_mem, sem.at[0])
     load.start()
+    half = attended_ref.shape[1]
     lines, _, span, hd = back_ref.shape
     parts, _, width = out_ref.shape
     strided = by_token(back_ref[:, 0].astype(F32).reshape(lines * span, hd).astype(BF16), heads)
+    cols = [slice(p * width, (p + 1) * width) for p in range(parts)]
+    sums = [mm(strided, w_ref[half:, c]) for c in cols]
     load.wait()
-    attended = jnp.concatenate([attended_mem[...], strided], axis=1)
-    for p in range(parts):
-        out_ref[p] = mm(attended, w_ref[:, p * width : (p + 1) * width]).astype(BF16)
-
-
-def finish_kernel(sums_ref, dq_ref, mid_ref, *refs):
-    *returns, back_ref, mixed_ref, grads_ref = refs
+    for p, c in enumerate(cols):
+        out_ref[p] = (sums[p] + mm(attended_mem[...], w_ref[:half, c])).astype(BF16)
+
+
+def finish_kernel(
+    heads, sums_ref, dq_ref, mid_ref, d_ref, e_ref, f_ref, back_ref, mixed_ref, grads_ref
+):
     mixed_ref[...] = sum(sums_ref[p].astype(F32) for p in range(sums_ref.shape[0])).astype(BF16)
     rows, hd = dq_ref.shape
-    grads_ref[0, 0] = dq_ref[...]
+    pieces = [dq_ref[...]]
     for kind in range(2):
-        total = mid_ref[kind].astype(F32) + sum(r[kind].astype(F32) for r in returns)
-        grads_ref[0, 1 + kind] = total.astype(BF16)
+        total = mid_ref[kind].astype(F32) + d_ref[0, kind].astype(F32)
+        total = total + e_ref[kind].astype(F32) + f_ref[kind].astype(F32)
+        pieces.append(total.astype(BF16))
+    joined = mm_tn(places(rows, heads), jnp.concatenate(pieces, axis=1)).astype(BF16)
     for kind in range(3):
+        grads_ref[0, kind] = joined[:, kind * hd : (kind + 1) * hd]
         grads_ref[1, kind] = back_ref[:, 1 + kind].astype(F32).reshape(rows, hd).astype(BF16)
 
 
@@ -239,10 +262,17 @@
     x = qkv.reshape(2, 3, rows, hd)
     w = out_weight.reshape(2 * heads * hd, parts * width)
 
-    pair = x[0, 1:3]
+    flat, pair_of, wide = (rows, hd), (2, rows, hd), (tokens, heads * hd)
+    pair, query = call(
+        kernel(split_kernel, heads),
+        [(pair_of, BF16), (flat, BF16)],
+        x,
+        far=(0,),
+        scratch=(((3, *flat), BF16), 1),
+    )
     a = shifted(pair, 2)
     og = lax.all_gather(out_grad, "head", axis=0)
-    both = jnp.stack([lax.optimization_barrier((x, a))[0][0, 1:3], a])
+    both = jnp.stack([pair, a])
     b = shifted(both, 1)
     c = shifted(a, 2)
     (send,) = call(
@@ -256,24 +286,29 @@
     )
     got = lax.all_to_all(send, "line", 0, 0, tiled=True)
     flat, pair_of = (rows, hd), (2, rows, hd)
-    flat, pair_of, wide = (rows, hd), (2, rows, hd), (tokens, heads * hd)
-    away = (wide, flat, pair_of, pair_of, pair_of)
-    three, four, attended, local_dq, mid, two, one = call(
+    (g_local,) = call(kernel(local_grad_kernel, heads), [(flat, BF16)], og, w)
+    away = (wide, flat, pair_of, pair_of)
+    one_three, four, attended, local_dq, mid, two = call(
         kernel(local_kernel, heads, scale),
-        [(o, BF16) for o in (pair_of, pair_of, *away)],
+        [(o, BF16) for o in ((2, *pair_of), pair_of, *away)],
         rank.reshape(1),
-        x,
-        og,
-        w,
+        query,
+        pair,
+        g_local,
         a,
         b,
         c,
-        away=(2, 3, 4, 5, 6),
+        away=(2, 3, 4, 5),
         scratch=(*((o, BF16) for o in away), len(away)),
     )
-    returns = [shifted(v, -n) for n, v in ((1, one), (2, two), (3, three), (4, four))]
+    d = shifted(one_three, -1)
+    e = shifted(four, -4)
     (results,) = call(kernel(strided_kernel, scale), [(got.shape, BF16)], got)
     returned = lax.all_to_all(results, "line", 0, 0, tiled=True)
+    (twos,) = call(
+        combine_kernel, [(pair_of, BF16)], two, d, far=(0,), scratch=((pair_of, BF16), 1)
+    )
+    f = shifted(twos, -2)
     (partial,) = call(
         kernel(project_kernel, heads),
         [((parts, tokens, width), BF16)],
@@ -285,12 +320,14 @@
     )
     sums = lax.all_to_all(partial, "head", 0, 0, tiled=True)
     mixed, grads = call(
-        finish_kernel,
+        kernel(finish_kernel, heads),
         [((tokens, width), BF16), ((2, 3, rows, hd), BF16)],
         sums,
         local_dq,
         mid,
-        *returns,
+        d,
+        e,
+        f,
         returned,
     )
     return mixed, grads.reshape(qkv.shape)

time: 119 us -> 109 us (0.916)
  the two profiles are of different devices: /device:TPU:62 before, /device:TPU:55 now
where the time goes in v1:
time: 109 us; the launch traced here: 108 us
  starting transfers between devices  57.5 us (53%)
  waiting for transfers between devices  26.2 us (24%)
  Pallas kernels  14.8 us (14%)
  blocking collectives  7.49 us (7%)
    ppermute x6, starting transfers between devices, shifted(): return lax.ppermute(value, seq, pairs)  23.3 us
    ppermute x6, waiting for transfers between devices, shifted(): return lax.ppermute(value, seq, pairs)  20 us
    all_to_all x1, starting transfers between devices, layer(): got = lax.all_to_all(send, 'line', 0, 0, tiled=True)  17.7 us
    pallas_call x8, Pallas kernels, call(): pl.pallas_call(kernel, out_shape=made, in_specs=ins, out_specs=[hbm if n...  14.8 us
    all_to_all x1, starting transfers between devices, layer(): returned = lax.all_to_all(results, 'line', 0, 0, tiled=True)  10.5 us
    all_gather x1, blocking collectives, layer(): og = lax.all_gather(out_grad, 'head', axis=0)  7.49 us
    all_to_all x1, waiting for transfers between devices, layer(): got = lax.all_to_all(send, 'line', 0, 0, tiled=True)  6.26 us
    all_to_all x1, starting transfers between devices, layer(): sums = lax.all_to_all(partial, 'head', 0, 0, tiled=True)  6.03 us
  transfers between devices with their start and end apart: 9, of which 4 were waited for; matrix products, arithmetic and copies ran while one was open for 1% of the time, Pallas kernels for 10%

profile of v1, /device:TPU:55, one launch (start us, length us, event | category | flops | bytes accessed | tf_op | source)
XLA Modules:
  0.0 108.3 jit_solution(6321875940236503953)
XLA Ops:
  0.6 7.5 %all-gather = bf16[512,512]{1,0:T(8,128)(2,1)S(1)} all-gather(bf16[128,512]{1,0:T(8,128)(2,1)} %param.5), channel_id=2, replica_groups=mesh['line'=32,'quarter'=4,'head'=4] {'head'}, dimensions={0}, use_global_device_ids=true | all-gather | bytes 655360 | tf_op jit(solution)/shard_map/all_gather | solution.py:274
  8.1 0.0 copy-start
  8.1 3.2 %shard_map.53 = bf16[32,4,8,128]{3,2,1,0:T(8,128)(2,1)} custom-call(bf16[4,128,512]{2,1,0:T(8,128)(2,1)S(1)} %bitcast.10, bf16[512,2048]{1,0:T(8,128)(2,1)} %bitcast.7, bf16[2,3,256,128]{3,2,1,0:T(8,128)(2,1)} %bitcast.14), custom_call_target="tpu_custom_call" | custom-call | tf_op jit(solution)/shard_map/pallas_call | solution.py:232
  11.4 17.7 %all-to-all-start = ((bf16[32,4,8,128]{3,2,1,0:T(8,128)(2,1)}), bf16[32,4,8,128]{3,2,1,0:T(8,128)(2,1)S(1)}, u32[]{:S(2)}, u32[]{:S(2)}) async-start(bf16[32,4,8,128]{3,2,1,0:T(8,128)(2,1)} %shard_map.53), calls=%async_computation | async-start | bytes 524288 | tf_op jit(solution)/shard_map/all_to_all | solution.py:287
  29.1 1.2 %shard_map.50 = (bf16[2,256,128]{2,1,0:T(8,128)(2,1)S(1)}, bf16[256,128]{1,0:T(8,128)(2,1)S(1)}) custom-call(bf16[2,3,256,128]{3,2,1,0:T(8,128)(2,1)} %bitcast.15), custom_call_target="tpu_custom_call" | custom-call | tf_op jit(solution)/shard_map/pallas_call | solution.py:232
  30.2 2.9 %collective-permute-start = (bf16[2,256,128]{2,1,0:T(8,128)(2,1)S(1)}, bf16[2,256,128]{2,1,0:T(8,128)(2,1)S(1)}, u32[]{:S(2)}, u32[]{:S(2)}) collective-permute-start(bf16[2,256,128]{2,1,0:T(8,128)(2,1)S(1)} %get-tuple-element.13.pair_ref), channel_id=1, source_target_pairs={{0,8},{4,12},{8,16},{12,20},{16,24},{20,28},{24,32},{28,36},{32,40... | collective-permute-start | bytes 393224 | tf_op jit(solution)/shard_map/ppermute | solution.py:260
  33.1 6.3 %all-to-all-done.in_ref = bf16[32,4,8,128]{3,2,1,0:T(8,128)(2,1)S(1)} async-done(((bf16[32,4,8,128]{3,2,1,0:T(8,128)(2,1)}), bf16[32,4,8,128]{3,2,1,0:T(8,128)(2,1)S(1)}, u32[]{:S(2)}, u32[]{:S(2)}) %all-to-all-start) | async-done | bytes 262176 | tf_op jit(solution)/shard_map/all_to_all | solution.py:287
  39.4 1.6 %shard_map.54 = bf16[32,4,8,128]{3,2,1,0:T(8,128)(2,1)} custom-call(bf16[32,4,8,128]{3,2,1,0:T(8,128)(2,1)S(1)} %all-to-all-done.in_ref), custom_call_target="tpu_custom_call" | custom-call | tf_op jit(solution)/shard_map/pallas_call | solution.py:232
  40.9 10.5 %all-to-all-start.1 = ((bf16[32,4,8,128]{3,2,1,0:T(8,128)(2,1)}), bf16[32,4,8,128]{3,2,1,0:T(8,128)(2,1)S(1)}, u32[]{:S(2)}, u32[]{:S(2)}) async-start(bf16[32,4,8,128]{3,2,1,0:T(8,128)(2,1)} %shard_map.54), calls=%async_computation.1 | async-start | bytes 524288 | tf_op jit(solution)/shard_map/all_to_all | solution.py:307
  51.4 0.0 collective-permute-done.a_ref
  51.4 0.7 pad_maximum_fusion
  52.2 2.6 %collective-permute-start.1 = (bf16[2,2,256,128]{3,2,1,0:T(8,128)(2,1)}, bf16[2,2,256,128]{3,2,1,0:T(8,128)(2,1)S(1)}, u32[]{:S(2)}, u32[]{:S(2)}) collective-permute-start(bf16[2,2,256,128]{3,2,1,0:T(8,128)(2,1)} %pad_maximum_fusion), channel_id=1, source_target_pairs={{0,4},{4,8},{8,12},{12,16},{16,20},{20,24},{24,28},{28,32},{32,36}... | collective-permute-start | bytes 786440 | tf_op jit(solution)/shard_map/ppermute | solution.py:260
  54.8 4.4 %collective-permute-start.2 = (bf16[2,256,128]{2,1,0:T(8,128)(2,1)S(1)}, bf16[2,256,128]{2,1,0:T(8,128)(2,1)}, u32[]{:S(2)}, u32[]{:S(2)}) collective-permute-start(bf16[2,256,128]{2,1,0:T(8,128)(2,1)S(1)} %collective-permute-done.a_ref), channel_id=1, source_target_pairs={{0,8},{4,12},{8,16},{12,20},{16,24},{20,28},{24,32},{28,36},{32,40... | collective-permute-start | bytes 393224 | tf_op jit(solution)/shard_map/ppermute | solution.py:260
  59.1 0.0 copy-done
  59.1 0.6 shard_map.51.g_ref
  59.8 7.6 %collective-permute-done.2.c_ref = bf16[2,256,128]{2,1,0:T(8,128)(2,1)} collective-permute-done((bf16[2,256,128]{2,1,0:T(8,128)(2,1)S(1)}, bf16[2,256,128]{2,1,0:T(8,128)(2,1)}, u32[]{:S(2)}, u32[]{:S(2)}) %collective-permute-start.2) | collective-permute-done | bytes 131104 | tf_op jit(solution)/shard_map/ppermute | solution.py:260
  67.4 0.0 collective-permute-done.1.b_ref
  67.4 4.0 %shard_map.52 = (bf16[2,2,256,128]{3,2,1,0:T(8,128)(2,1)}, bf16[2,256,128]{2,1,0:T(8,128)(2,1)S(1)}, bf16[128,256]{1,0:T(8,128)(2,1)}, bf16[256,128]{1,0:T(8,128...) custom-call(s32[1]{0:T(128)} %bitcast.rank_ref, bf16[256,128]{1,0:T(8,128)(2,1)S(1)} %get-tuple-element.12.query_ref, ...), custom_call_target="tpu_custom_call" | custom-call | tf_op jit(solution)/shard_map/pallas_call | solution.py:232
  71.4 0.0 copy-start.3
  71.4 0.6 copy-done.3
  72.1 0.0 copy-start.4
  72.1 5.2 %collective-permute-start.3 = (bf16[2,2,256,128]{3,2,1,0:T(8,128)(2,1)}, bf16[2,2,256,128]{3,2,1,0:T(8,128)(2,1)S(1)}, u32[]{:S(2)}, u32[]{:S(2)}) collective-permute-start(bf16[2,2,256,128]{3,2,1,0:T(8,128)(2,1)} %get-tuple-element.17), channel_id=1, source_target_pairs={{4,0},{8,4},{12,8},{16,12},{20,16},{24,20},{28,24},{32,28},{36,32}... | collective-permute-start | bytes 786440 | tf_op jit(solution)/shard_map/ppermute | solution.py:260
  77.3 0.0 all-to-all-done.1.back_ref
  77.3 0.0 copy-start.1
  77.3 0.0 copy-start.2
  77.3 2.2 %shard_map.55 = bf16[4,128,512]{2,1,0:T(8,128)(2,1)} custom-call(bf16[128,256]{1,0:T(8,128)(2,1)} %get-tuple-element.14.attended_ref, bf16[32,4,8,128]{3,2,1,0:T(8,128)(2,1)S(1)} %all-to-all-done.1.back_ref, bf16[512,2048]{1,0:T(8,128)(2,1)S(1)} %bitcast.9), custom_call_target="tpu_custom_call" | custom-call | tf_op jit(solution)/shard_map/pallas_call | solution.py:232
  79.5 6.0 %all-to-all-start.2 = ((bf16[4,128,512]{2,1,0:T(8,128)(2,1)}), bf16[4,128,512]{2,1,0:T(8,128)(2,1)S(1)}, u32[]{:S(2)}, u32[]{:S(2)}) async-start(bf16[4,128,512]{2,1,0:T(8,128)(2,1)} %shard_map.55), calls=%async_computation.2 | async-start | bytes 1048576 | tf_op jit(solution)/shard_map/all_to_all | solution.py:321
  85.5 0.0 copy-done.4
  85.5 6.1 %collective-permute-start.4 = (bf16[2,256,128]{2,1,0:T(8,128)(2,1)S(1)}, bf16[2,256,128]{2,1,0:T(8,128)(2,1)S(1)}, u32[]{:S(2)}, u32[]{:S(2)}) collective-permute-start(bf16[2,256,128]{2,1,0:T(8,128)(2,1)S(1)} %copy-done.4), channel_id=1, source_target_pairs={{16,0},{20,4},{24,8},{28,12},{32,16},{36,20},{40,24},{44,28},{48,3... | collective-permute-start | bytes 393224 | tf_op jit(solution)/shard_map/ppermute | solution.py:260
  91.6 0.0 collective-permute-done.3.d_ref
  91.6 0.9 shard_map.56
  92.5 2.2 %collective-permute-start.5 = (bf16[2,256,128]{2,1,0:T(8,128)(2,1)S(1)}, bf16[2,256,128]{2,1,0:T(8,128)(2,1)S(1)}, u32[]{:S(2)}, u32[]{:S(2)}) collective-permute-start(bf16[2,256,128]{2,1,0:T(8,128)(2,1)S(1)} %shard_map.56), channel_id=1, source_target_pairs={{8,0},{12,4},{16,8},{20,12},{24,16},{28,20},{32,24},{36,28},{40,32... | collective-permute-start | bytes 393224 | tf_op jit(solution)/shard_map/ppermute | solution.py:260
  94.7 7.7 %collective-permute-done.4.e_ref = bf16[2,256,128]{2,1,0:T(8,128)(2,1)S(1)} collective-permute-done((bf16[2,256,128]{2,1,0:T(8,128)(2,1)S(1)}, bf16[2,256,128]{2,1,0:T(8,128)(2,1)S(1)}, u32[]{:S(2)}, u32[]{:S(2)}) %collective-permute-start.4) | collective-permute-done | bytes 131104 | tf_op jit(solution)/shard_map/ppermute | solution.py:260
  102.5 4.6 %collective-permute-done.5.f_ref = bf16[2,256,128]{2,1,0:T(8,128)(2,1)S(1)} collective-permute-done((bf16[2,256,128]{2,1,0:T(8,128)(2,1)S(1)}, bf16[2,256,128]{2,1,0:T(8,128)(2,1)S(1)}, u32[]{:S(2)}, u32[]{:S(2)}) %collective-permute-start.5) | collective-permute-done | bytes 131104 | tf_op jit(solution)/shard_map/ppermute | solution.py:260
  107.1 0.0 all-to-all-done.2.sums_ref
  107.1 0.0 copy-done.1
  107.1 0.0 copy-done.2
  107.1 1.1 %shard_map.57 = (bf16[128,512]{1,0:T(8,128)(2,1)}, bf16[2,3,256,128]{3,2,1,0:T(8,128)(2,1)}) custom-call(bf16[4,128,512]{2,1,0:T(8,128)(2,1)S(1)} %all-to-all-done.2.sums_ref, bf16[256,128]{1,0:T(8,128)(2,1)S(1)} %copy-done.2, bf16[2,256,128]{2,1,0:T(8,128)(2,1)S(1)} %copy-done.1, bf16[2,2,256,128]{3,2,1,0:T(8,128)(2,1)S(1)} %collective-permute-done.3.d_ref, ...), custom_call_target="tpu_custom_call" | custom-call | tf_op jit(solution)/shard_map/pallas_call | solution.py:232
Async XLA Ops:
  8.1 51.0 %copy-start = (bf16[2,2,128,2048]{3,2,1,0:T(8,128)(2,1)S(1)}, bf16[2,2,128,2048]{3,2,1,0:T(8,128)(2,1)}, u32[]{:S(2)}) copy-start(bf16[2,2,128,2048]{3,2,1,0:T(8,128)(2,1)} %param.4) | copy-start | bytes 6291460
  11.4 28.0 %all-to-all-start = ((bf16[32,4,8,128]{3,2,1,0:T(8,128)(2,1)}), bf16[32,4,8,128]{3,2,1,0:T(8,128)(2,1)S(1)}, u32[]{:S(2)}, u32[]{:S(2)}) async-start(bf16[32,4,8,128]{3,2,1,0:T(8,128)(2,1)} %shard_map.53), calls=%async_computation | async-start | bytes 524288 | tf_op jit(solution)/shard_map/all_to_all | solution.py:287
  30.2 21.2 %collective-permute-start = (bf16[2,256,128]{2,1,0:T(8,128)(2,1)S(1)}, bf16[2,256,128]{2,1,0:T(8,128)(2,1)S(1)}, u32[]{:S(2)}, u32[]{:S(2)}) collective-permute-start(bf16[2,256,128]{2,1,0:T(8,128)(2,1)S(1)} %get-tuple-element.13.pair_ref), channel_id=1, source_target_pairs={{0,8},{4,12},{8,16},{12,20},{16,24},{20,28},{24,32},{28,36},{32,40... | collective-permute-start | bytes 393224 | tf_op jit(solution)/shard_map/ppermute | solution.py:260
  40.9 36.4 %all-to-all-start.1 = ((bf16[32,4,8,128]{3,2,1,0:T(8,128)(2,1)}), bf16[32,4,8,128]{3,2,1,0:T(8,128)(2,1)S(1)}, u32[]{:S(2)}, u32[]{:S(2)}) async-start(bf16[32,4,8,128]{3,2,1,0:T(8,128)(2,1)} %shard_map.54), calls=%async_computation.1 | async-start | bytes 524288 | tf_op jit(solution)/shard_map/all_to_all | solution.py:307
  52.2 15.2 %collective-permute-start.1 = (bf16[2,2,256,128]{3,2,1,0:T(8,128)(2,1)}, bf16[2,2,256,128]{3,2,1,0:T(8,128)(2,1)S(1)}, u32[]{:S(2)}, u32[]{:S(2)}) collective-permute-start(bf16[2,2,256,128]{3,2,1,0:T(8,128)(2,1)} %pad_maximum_fusion), channel_id=1, source_target_pairs={{0,4},{4,8},{8,12},{12,16},{16,20},{20,24},{24,28},{28,32},{32,36}... | collective-permute-start | bytes 786440 | tf_op jit(solution)/shard_map/ppermute | solution.py:260
  54.8 12.6 %collective-permute-start.2 = (bf16[2,256,128]{2,1,0:T(8,128)(2,1)S(1)}, bf16[2,256,128]{2,1,0:T(8,128)(2,1)}, u32[]{:S(2)}, u32[]{:S(2)}) collective-permute-start(bf16[2,256,128]{2,1,0:T(8,128)(2,1)S(1)} %collective-permute-done.a_ref), channel_id=1, source_target_pairs={{0,8},{4,12},{8,16},{12,20},{16,24},{20,28},{24,32},{28,36},{32,40... | collective-permute-start | bytes 393224 | tf_op jit(solution)/shard_map/ppermute | solution.py:260
  71.4 0.7 copy-start.3
  72.1 13.4 %copy-start.4 = (bf16[2,256,128]{2,1,0:T(8,128)(2,1)S(1)}, bf16[2,256,128]{2,1,0:T(8,128)(2,1)}, u32[]{:S(2)}) copy-start(bf16[2,256,128]{2,1,0:T(8,128)(2,1)} %copy-done.3) | copy-start | bytes 393220
  72.1 19.5 %collective-permute-start.3 = (bf16[2,2,256,128]{3,2,1,0:T(8,128)(2,1)}, bf16[2,2,256,128]{3,2,1,0:T(8,128)(2,1)S(1)}, u32[]{:S(2)}, u32[]{:S(2)}) collective-permute-start(bf16[2,2,256,128]{3,2,1,0:T(8,128)(2,1)} %get-tuple-element.17), channel_id=1, source_target_pairs={{4,0},{8,4},{12,8},{16,12},{20,16},{24,20},{28,24},{32,28},{36,32}... | collective-permute-start | bytes 786440 | tf_op jit(solution)/shard_map/ppermute | solution.py:260
  77.3 29.8 %copy-start.1 = (bf16[2,256,128]{2,1,0:T(8,128)(2,1)S(1)}, bf16[2,256,128]{2,1,0:T(8,128)(2,1)}, u32[]{:S(2)}) copy-start(bf16[2,256,128]{2,1,0:T(8,128)(2,1)} %get-tuple-element.16.mid_ref) | copy-start | bytes 393220
  77.3 29.8 %copy-start.2 = (bf16[256,128]{1,0:T(8,128)(2,1)S(1)}, bf16[256,128]{1,0:T(8,128)(2,1)}, u32[]{:S(2)}) copy-start(bf16[256,128]{1,0:T(8,128)(2,1)} %get-tuple-element.15.dq_ref) | copy-start | bytes 196612
  79.5 27.6 %all-to-all-start.2 = ((bf16[4,128,512]{2,1,0:T(8,128)(2,1)}), bf16[4,128,512]{2,1,0:T(8,128)(2,1)S(1)}, u32[]{:S(2)}, u32[]{:S(2)}) async-start(bf16[4,128,512]{2,1,0:T(8,128)(2,1)} %shard_map.55), calls=%async_computation.2 | async-start | bytes 1048576 | tf_op jit(solution)/shard_map/all_to_all | solution.py:321
  85.5 16.9 %collective-permute-start.4 = (bf16[2,256,128]{2,1,0:T(8,128)(2,1)S(1)}, bf16[2,256,128]{2,1,0:T(8,128)(2,1)S(1)}, u32[]{:S(2)}, u32[]{:S(2)}) collective-permute-start(bf16[2,256,128]{2,1,0:T(8,128)(2,1)S(1)} %copy-done.4), channel_id=1, source_target_pairs={{16,0},{20,4},{24,8},{28,12},{32,16},{36,20},{40,24},{44,28},{48,3... | collective-permute-start | bytes 393224 | tf_op jit(solution)/shard_map/ppermute | solution.py:260
  92.5 14.6 %collective-permute-start.5 = (bf16[2,256,128]{2,1,0:T(8,128)(2,1)S(1)}, bf16[2,256,128]{2,1,0:T(8,128)(2,1)S(1)}, u32[]{:S(2)}, u32[]{:S(2)}) collective-permute-start(bf16[2,256,128]{2,1,0:T(8,128)(2,1)S(1)} %shard_map.56), channel_id=1, source_target_pairs={{8,0},{12,4},{16,8},{20,12},{24,16},{28,20},{32,24},{36,28},{40,32... | collective-permute-start | bytes 393224 | tf_op jit(solution)/shard_map/ppermute | solution.py:260

commit v2 on v1

--- a/solution.py
+++ b/solution.py
@@ -35,15 +35,22 @@
     return lax.broadcasted_iota(jnp.int32, shape, axis)
 
 
-def attend(q, k, v, g, allowed, scale):
+def forward(q, k, v, allowed, scale):
     scores = jnp.where(allowed, mm_nt(q, k) * scale, -jnp.inf)
     largest = jnp.max(scores, axis=1, keepdims=True)
     raised = jnp.exp(scores - largest)
     probs = raised * (1.0 / jnp.sum(raised, axis=1, keepdims=True))
-    rounded = probs.astype(BF16)
-    out = mm(rounded, v).astype(BF16)
+    return probs, probs.astype(BF16), mm(probs.astype(BF16), v).astype(BF16)
+
+
+def score_grads(probs, out, v, g):
     delta = jnp.sum(g.astype(F32) * out.astype(F32), axis=1, keepdims=True)
-    gs = (probs * (mm_nt(g, v) - delta)).astype(BF16)
+    return (probs * (mm_nt(g, v) - delta)).astype(BF16)
+
+
+def attend(q, k, v, g, allowed, scale):
+    probs, rounded, out = forward(q, k, v, allowed, scale)
+    gs = score_grads(probs, out, v, g)
     return out, mm(gs, k) * scale, mm_tn(gs, q) * scale, mm_tn(rounded, g)
 
 
@@ -55,27 +62,14 @@
     return total
 
 
-def grad_heads_kernel(heads, og_ref, w_ref, x_ref, send_ref, w_mem, x_mem, sems):
+def grad_heads_kernel(heads, og_ref, w_ref, x_ref, send_ref):
     lines, _, span, hd = send_ref.shape
-    parts, tokens, width = og_ref.shape
-    loads = [
-        pltpu.make_async_copy(
-            w_ref.at[heads * hd :, p * width : (p + 1) * width], w_mem.at[p], sems.at[p]
-        )
-        for p in range(parts)
-    ]
-    loads.append(pltpu.make_async_copy(x_ref.at[1], x_mem, sems.at[parts]))
-    for load in loads:
-        load.start()
-    loads[parts].wait()
-    for kind in range(3):
-        send_ref[:, kind] = x_mem[kind].astype(F32).reshape(lines, span, hd).astype(BF16)
-    g = 0
-    for p in range(parts):
-        loads[p].wait()
-        g = g + mm_nt(w_mem[p], og_ref[p])
+    parts, tokens, _ = og_ref.shape
+    g = sum(mm_nt(w_ref[p], og_ref[p]) for p in range(parts))
     g = rows_of(g.astype(BF16), lines * span, heads, hd, tokens)
     send_ref[:, 3] = g.reshape(lines, span, hd).astype(BF16)
+    for kind in range(3):
+        send_ref[:, kind] = x_ref[kind].astype(F32).reshape(lines, span, hd).astype(BF16)
 
 
 def strided_kernel(scale, in_ref, out_ref):
@@ -105,9 +99,16 @@
     return (iota((rows, rows), 1) == at % tokens * heads + at // tokens).astype(BF16)
 
 
-def split_kernel(heads, x_ref, pair_ref, query_ref, x_mem, sem):
-    load = pltpu.make_async_copy(x_ref.at[0], x_mem, sem.at[0])
+def split_kernel(heads, x_ref, w_ref, pair_ref, query_ref, w_out, x_out, x_mem, sems):
+    parts, half, width = w_out.shape
+    load = pltpu.make_async_copy(x_ref.at[0], x_mem, sems.at[0])
+    others = [pltpu.make_async_copy(x_ref.at[1], x_out, sems.at[1])]
+    for p in range(parts):
+        cols = slice(p * width, (p + 1) * width)
+        others.append(pltpu.make_async_copy(w_ref.at[half:, cols], w_out.at[p], sems.at[2 + p]))
     load.start()
+    for other in others:
+        other.start()
     rows, hd = query_ref.shape
     apart = places(rows, heads)
     load.wait()
@@ -115,6 +116,8 @@
     query_ref[...] = whole[:, :hd]
     pair_ref[0] = whole[:, hd : 2 * hd]
     pair_ref[1] = whole[:, 2 * hd :]
+    for other in others:
+        other.wait()
 
 
 def local_grad_kernel(heads, og_ref, w_ref, g_ref):
@@ -142,35 +145,6 @@
     gap = iota((tokens, 1), 0) + back * tokens - to
     first = (back - rank_ref[0]) * tokens
     allowed = (gap >= 0) & (gap < ROW) & (to >= first)
-    outs = []
-    for h in range(heads):
-        mine = slice(h * tokens, (h + 1) * tokens)
-
-        def window(kind):
-            return jnp.concatenate(
-                [
-                    c_ref[kind, mine],
-                    b_ref[1, kind, mine],
-                    a_ref[kind, mine],
-                    b_ref[0, kind, mine],
-                    pair_ref[kind, mine],
-                ],
-                axis=0,
-            )
-
-        out, dq, *pair = attend(query_ref[mine], window(0), window(1), g_ref[mine], allowed, scale)
-        outs.append(out)
-        dq_mem[mine] = dq.astype(BF16)
-        for kind, value in enumerate(pair):
-            four, three, two, one, mid = [
-                value[j * tokens : (j + 1) * tokens].astype(BF16) for j in range(back + 1)
-            ]
-            mid_mem[kind, mine] = mid
-            two_mem[kind, mine] = two
-            one_three_ref[0, kind, mine] = one
-            one_three_ref[1, kind, mine] = three
-            four_ref[kind, mine] = four
-    attended_mem[...] = jnp.concatenate(outs, axis=1)
     pairs = (
         (attended_mem, attended_ref),
         (dq_mem, dq_ref),
@@ -178,8 +152,43 @@
         (two_mem, two_ref),
     )
     stores = [pltpu.make_async_copy(m, r, sems.at[n]) for n, (m, r) in enumerate(pairs)]
-    for store in stores:
-        store.start()
+    slices = [slice(h * tokens, (h + 1) * tokens) for h in range(heads)]
+
+    def window(kind, mine):
+        refs = (c_ref, b_ref.at[1], a_ref, b_ref.at[0], pair_ref)
+        return jnp.concatenate([r[kind, mine] for r in refs], axis=0)
+
+    keys = [window(0, mine) for mine in slices]
+    values = [window(1, mine) for mine in slices]
+    ran = [
+        forward(query_ref[mine], k, v, allowed, scale) for mine, k, v in zip(slices, keys, values)
+    ]
+    attended_mem[...] = jnp.concatenate([r[2] for r in ran], axis=1)
+    stores[0].start()
+    grads = [
+        score_grads(r[0], r[2], v, g_ref[mine]) for mine, r, v in zip(slices, ran, values)
+    ]
+
+    def block(j, h, kind):
+        cols = slice(j * tokens, (j + 1) * tokens)
+        if kind == 0:
+            return (mm_tn(grads[h][:, cols], query_ref[slices[h]]) * scale).astype(BF16)
+        return mm_tn(ran[h][1][:, cols], g_ref[slices[h]]).astype(BF16)
+
+    for h, mine in enumerate(slices):
+        for kind in range(2):
+            mid_mem[kind, mine] = block(back, h, kind)
+            two_mem[kind, mine] = block(back - 2, h, kind)
+    stores[2].start()
+    stores[3].start()
+    for h, mine in enumerate(slices):
+        dq_mem[mine] = (mm(grads[h], keys[h]) * scale).astype(BF16)
+    stores[1].start()
+    for h, mine in enumerate(slices):
+        for kind in range(2):
+            one_three_ref[0, kind, mine] = block(back - 1, h, kind)
+            one_three_ref[1, kind, mine] = block(back - 3, h, kind)
+            four_ref[kind, mine] = block(back - 4, h, kind)
     for store in stores:
         store.wait()
 
@@ -263,12 +272,18 @@
     w = out_weight.reshape(2 * heads * hd, parts * width)
 
     flat, pair_of, wide = (rows, hd), (2, rows, hd), (tokens, heads * hd)
-    pair, query = call(
+    pair, query, w_strided, x_strided = call(
         kernel(split_kernel, heads),
-        [(pair_of, BF16), (flat, BF16)],
+        [
+            (pair_of, BF16),
+            (flat, BF16),
+            ((parts, heads * hd, width), BF16),
+            ((3, *flat), BF16),
+        ],
         x,
-        far=(0,),
-        scratch=(((3, *flat), BF16), 1),
+        w,
+        far=(0, 1),
+        scratch=(((3, *flat), BF16), 2 + parts),
     )
     a = shifted(pair, 2)
     og = lax.all_gather(out_grad, "head", axis=0)
@@ -276,13 +291,7 @@
     b = shifted(both, 1)
     c = shifted(a, 2)
     (send,) = call(
-        kernel(grad_heads_kernel, heads),
-        [((lines, 4, span, hd), BF16)],
-        og,
-        w,
-        x,
-        far=(1, 2),
-        scratch=(((parts, heads * hd, width), BF16), ((3, rows, hd), BF16), parts + 1),
+        kernel(grad_heads_kernel, heads), [((lines, 4, span, hd), BF16)], og, w_strided, x_strided
     )
     got = lax.all_to_all(send, "line", 0, 0, tiled=True)
     flat, pair_of = (rows, hd), (2, rows, hd)

time: 109 us -> 108 us (level)
  waiting for transfers between devices: 26.2 us -> 28.1 us
  Pallas kernels: 14.8 us -> 12.9 us
    pallas_call x8, Pallas kernels: 14.8 us -> 12.9 us  [call(): pl.pallas_call(kernel, out_shape=made, in_specs=ins, out_specs=[hbm if n...]
    all_to_all x1, waiting for transfers between devices: 6.26 us -> 7.42 us  [layer(): got = lax.all_to_all(send, 'line', 0, 0, tiled=True)]
  transfers between devices with their start and end apart: 9 -> 9, of which waited for: 4 -> 4; matrix products, arithmetic and copies ran while one was open for 1% -> 1% of each run, Pallas kernels for 10% -> 8%
where the time goes in v2:
time: 108 us
  starting transfers between devices  57 us (53%)
  waiting for transfers between devices  28.1 us (26%)
  Pallas kernels  12.9 us (12%)
  blocking collectives  7.49 us (7%)
    ppermute x6, starting transfers between devices, shifted(): return lax.ppermute(value, seq, pairs)  23 us
    ppermute x6, waiting for transfers between devices, shifted(): return lax.ppermute(value, seq, pairs)  20.7 us
    all_to_all x1, starting transfers between devices, layer(): got = lax.all_to_all(send, 'line', 0, 0, tiled=True)  17.7 us
    pallas_call x8, Pallas kernels, call(): pl.pallas_call(kernel, out_shape=made, in_specs=ins, out_specs=[hbm if n...  12.9 us
    all_to_all x1, starting transfers between devices, layer(): returned = lax.all_to_all(results, 'line', 0, 0, tiled=True)  9.92 us
    all_gather x1, blocking collectives, layer(): og = lax.all_gather(out_grad, 'head', axis=0)  7.49 us
    all_to_all x1, waiting for transfers between devices, layer(): got = lax.all_to_all(send, 'line', 0, 0, tiled=True)  7.42 us
    all_to_all x1, starting transfers between devices, layer(): sums = lax.all_to_all(partial, 'head', 0, 0, tiled=True)  6.39 us
  transfers between devices with their start and end apart: 9, of which 4 were waited for; matrix products, arithmetic and copies ran while one was open for 1% of the time, Pallas kernels for 8%

profile of v2, /device:TPU:55, one launch (start us, length us, event | category | flops | bytes accessed | tf_op | source)
XLA Modules:
  0.0 107.7 jit_solution(13083453763351768299)
XLA Ops:
  0.6 7.5 %all-gather = bf16[512,512]{1,0:T(8,128)(2,1)S(1)} all-gather(bf16[128,512]{1,0:T(8,128)(2,1)} %param.5), channel_id=2, replica_groups=mesh['line'=32,'quarter'=4,'head'=4] {'head'}, dimensions={0}, use_global_device_ids=true | all-gather | bytes 655360 | tf_op jit(solution)/shard_map/all_gather | solution.py:289
  8.1 1.4 %shard_map.50 = (bf16[2,256,128]{2,1,0:T(8,128)(2,1)S(1)}, bf16[256,128]{1,0:T(8,128)(2,1)S(1)}, bf16[4,256,512]{2,1,0:T(8,128)(2,1)S(1)}, bf16[3,256,128]{2,1,0:T(8,128)(2,1)S(1)}) custom-call(bf16[2,3,256,128]{3,2,1,0:T(8,128)(2,1)} %bitcast.14, bf16[512,2048]{1,0:T(8,128)(2,1)} %bitcast.7), custom_call_target="tpu_custom_call" | custom-call | tf_op jit(solution)/shard_map/pallas_call | solution.py:241
  9.6 0.0 copy-start
  9.6 1.4 %shard_map.53 = bf16[32,4,8,128]{3,2,1,0:T(8,128)(2,1)} custom-call(bf16[4,128,512]{2,1,0:T(8,128)(2,1)S(1)} %bitcast.10, bf16[4,256,512]{2,1,0:T(8,128)(2,1)S(1)} %get-tuple-element.17.w_ref, bf16[3,256,128]{2,1,0:T(8,128)(2,1)S(1)} %get-tuple-element.18.x_ref), custom_call_target="tpu_custom_call" | custom-call | tf_op jit(solution)/shard_map/pallas_call | solution.py:241
  10.9 17.7 %all-to-all-start = ((bf16[32,4,8,128]{3,2,1,0:T(8,128)(2,1)}), bf16[32,4,8,128]{3,2,1,0:T(8,128)(2,1)S(1)}, u32[]{:S(2)}, u32[]{:S(2)}) async-start(bf16[32,4,8,128]{3,2,1,0:T(8,128)(2,1)} %shard_map.53), calls=%async_computation | async-start | bytes 524288 | tf_op jit(solution)/shard_map/all_to_all | solution.py:296
  28.6 2.9 %collective-permute-start = (bf16[2,256,128]{2,1,0:T(8,128)(2,1)S(1)}, bf16[2,256,128]{2,1,0:T(8,128)(2,1)S(1)}, u32[]{:S(2)}, u32[]{:S(2)}) collective-permute-start(bf16[2,256,128]{2,1,0:T(8,128)(2,1)S(1)} %get-tuple-element.15.pair_ref), channel_id=1, source_target_pairs={{0,8},{4,12},{8,16},{12,20},{16,24},{20,28},{24,32},{28,36},{32,40... | collective-permute-start | bytes 393224 | tf_op jit(solution)/shard_map/ppermute | solution.py:269
  31.5 7.4 %all-to-all-done.in_ref = bf16[32,4,8,128]{3,2,1,0:T(8,128)(2,1)S(1)} async-done(((bf16[32,4,8,128]{3,2,1,0:T(8,128)(2,1)}), bf16[32,4,8,128]{3,2,1,0:T(8,128)(2,1)S(1)}, u32[]{:S(2)}, u32[]{:S(2)}) %all-to-all-start) | async-done | bytes 262176 | tf_op jit(solution)/shard_map/all_to_all | solution.py:296
  38.9 1.6 %shard_map.54 = bf16[32,4,8,128]{3,2,1,0:T(8,128)(2,1)} custom-call(bf16[32,4,8,128]{3,2,1,0:T(8,128)(2,1)S(1)} %all-to-all-done.in_ref), custom_call_target="tpu_custom_call" | custom-call | tf_op jit(solution)/shard_map/pallas_call | solution.py:241
  40.5 9.9 %all-to-all-start.1 = ((bf16[32,4,8,128]{3,2,1,0:T(8,128)(2,1)}), bf16[32,4,8,128]{3,2,1,0:T(8,128)(2,1)S(1)}, u32[]{:S(2)}, u32[]{:S(2)}) async-start(bf16[32,4,8,128]{3,2,1,0:T(8,128)(2,1)} %shard_map.54), calls=%async_computation.1 | async-start | bytes 524288 | tf_op jit(solution)/shard_map/all_to_all | solution.py:316
  50.4 0.0 collective-permute-done.a_ref
  50.4 0.7 pad_maximum_fusion
  51.2 3.2 %collective-permute-start.1 = (bf16[2,2,256,128]{3,2,1,0:T(8,128)(2,1)}, bf16[2,2,256,128]{3,2,1,0:T(8,128)(2,1)S(1)}, u32[]{:S(2)}, u32[]{:S(2)}) collective-permute-start(bf16[2,2,256,128]{3,2,1,0:T(8,128)(2,1)} %pad_maximum_fusion), channel_id=1, source_target_pairs={{0,4},{4,8},{8,12},{12,16},{16,20},{20,24},{24,28},{28,32},{32,36}... | collective-permute-start | bytes 786440 | tf_op jit(solution)/shard_map/ppermute | solution.py:269
  54.3 4.8 %collective-permute-start.2 = (bf16[2,256,128]{2,1,0:T(8,128)(2,1)S(1)}, bf16[2,256,128]{2,1,0:T(8,128)(2,1)}, u32[]{:S(2)}, u32[]{:S(2)}) collective-permute-start(bf16[2,256,128]{2,1,0:T(8,128)(2,1)S(1)} %collective-permute-done.a_ref), channel_id=1, source_target_pairs={{0,8},{4,12},{8,16},{12,20},{16,24},{20,28},{24,32},{28,36},{32,40... | collective-permute-start | bytes 393224 | tf_op jit(solution)/shard_map/ppermute | solution.py:269
  59.1 0.0 copy-done
  59.1 0.6 shard_map.51.g_ref
  59.8 8.2 %collective-permute-done.2.c_ref = bf16[2,256,128]{2,1,0:T(8,128)(2,1)} collective-permute-done((bf16[2,256,128]{2,1,0:T(8,128)(2,1)S(1)}, bf16[2,256,128]{2,1,0:T(8,128)(2,1)}, u32[]{:S(2)}, u32[]{:S(2)}) %collective-permute-start.2) | collective-permute-done | bytes 131104 | tf_op jit(solution)/shard_map/ppermute | solution.py:269
  68.0 0.0 collective-permute-done.1.b_ref
  68.0 3.6 %shard_map.52 = (bf16[2,2,256,128]{3,2,1,0:T(8,128)(2,1)}, bf16[2,256,128]{2,1,0:T(8,128)(2,1)S(1)}, bf16[128,256]{1,0:T(8,128)(2,1)}, bf16[256,128]{1,0:T(8,128...) custom-call(s32[1]{0:T(128)} %bitcast.rank_ref, bf16[256,128]{1,0:T(8,128)(2,1)S(1)} %get-tuple-element.14.query_ref, ...), custom_call_target="tpu_custom_call" | custom-call | tf_op jit(solution)/shard_map/pallas_call | solution.py:241
  71.7 0.0 copy-start.3
  71.7 0.6 copy-done.3
  72.3 0.0 copy-start.4
  72.3 4.0 %collective-permute-start.3 = (bf16[2,2,256,128]{3,2,1,0:T(8,128)(2,1)}, bf16[2,2,256,128]{3,2,1,0:T(8,128)(2,1)S(1)}, u32[]{:S(2)}, u32[]{:S(2)}) collective-permute-start(bf16[2,2,256,128]{3,2,1,0:T(8,128)(2,1)} %get-tuple-element.21), channel_id=1, source_target_pairs={{4,0},{8,4},{12,8},{16,12},{20,16},{24,20},{28,24},{32,28},{36,32}... | collective-permute-start | bytes 786440 | tf_op jit(solution)/shard_map/ppermute | solution.py:269
  76.4 0.0 all-to-all-done.1.back_ref
  76.4 0.0 copy-start.1
  76.4 0.0 copy-start.2
  76.4 2.2 %shard_map.55 = bf16[4,128,512]{2,1,0:T(8,128)(2,1)} custom-call(bf16[128,256]{1,0:T(8,128)(2,1)} %get-tuple-element.16.attended_ref, bf16[32,4,8,128]{3,2,1,0:T(8,128)(2,1)S(1)} %all-to-all-done.1.back_ref, bf16[512,2048]{1,0:T(8,128)(2,1)S(1)} %bitcast.9), custom_call_target="tpu_custom_call" | custom-call | tf_op jit(solution)/shard_map/pallas_call | solution.py:241
  78.6 6.4 %all-to-all-start.2 = ((bf16[4,128,512]{2,1,0:T(8,128)(2,1)}), bf16[4,128,512]{2,1,0:T(8,128)(2,1)S(1)}, u32[]{:S(2)}, u32[]{:S(2)}) async-start(bf16[4,128,512]{2,1,0:T(8,128)(2,1)} %shard_map.55), calls=%async_computation.2 | async-start | bytes 1048576 | tf_op jit(solution)/shard_map/all_to_all | solution.py:330
  85.0 0.0 copy-done.4
  85.0 6.1 %collective-permute-start.4 = (bf16[2,256,128]{2,1,0:T(8,128)(2,1)S(1)}, bf16[2,256,128]{2,1,0:T(8,128)(2,1)S(1)}, u32[]{:S(2)}, u32[]{:S(2)}) collective-permute-start(bf16[2,256,128]{2,1,0:T(8,128)(2,1)S(1)} %copy-done.4), channel_id=1, source_target_pairs={{16,0},{20,4},{24,8},{28,12},{32,16},{36,20},{40,24},{44,28},{48,3... | collective-permute-start | bytes 393224 | tf_op jit(solution)/shard_map/ppermute | solution.py:269
  91.0 0.0 collective-permute-done.3.d_ref
  91.0 0.9 shard_map.56
  92.0 2.1 %collective-permute-start.5 = (bf16[2,256,128]{2,1,0:T(8,128)(2,1)S(1)}, bf16[2,256,128]{2,1,0:T(8,128)(2,1)S(1)}, u32[]{:S(2)}, u32[]{:S(2)}) collective-permute-start(bf16[2,256,128]{2,1,0:T(8,128)(2,1)S(1)} %shard_map.56), channel_id=1, source_target_pairs={{8,0},{12,4},{16,8},{20,12},{24,16},{28,20},{32,24},{36,28},{40,32... | collective-permute-start | bytes 393224 | tf_op jit(solution)/shard_map/ppermute | solution.py:269
  94.1 7.9 %collective-permute-done.4.e_ref = bf16[2,256,128]{2,1,0:T(8,128)(2,1)S(1)} collective-permute-done((bf16[2,256,128]{2,1,0:T(8,128)(2,1)S(1)}, bf16[2,256,128]{2,1,0:T(8,128)(2,1)S(1)}, u32[]{:S(2)}, u32[]{:S(2)}) %collective-permute-start.4) | collective-permute-done | bytes 131104 | tf_op jit(solution)/shard_map/ppermute | solution.py:269
  102.0 4.5 %collective-permute-done.5.f_ref = bf16[2,256,128]{2,1,0:T(8,128)(2,1)S(1)} collective-permute-done((bf16[2,256,128]{2,1,0:T(8,128)(2,1)S(1)}, bf16[2,256,128]{2,1,0:T(8,128)(2,1)S(1)}, u32[]{:S(2)}, u32[]{:S(2)}) %collective-permute-start.5) | collective-permute-done | bytes 131104 | tf_op jit(solution)/shard_map/ppermute | solution.py:269
  106.5 0.0 all-to-all-done.2.sums_ref
  106.5 0.0 copy-done.1
  106.5 0.0 copy-done.2
  106.5 1.1 %shard_map.57 = (bf16[128,512]{1,0:T(8,128)(2,1)}, bf16[2,3,256,128]{3,2,1,0:T(8,128)(2,1)}) custom-call(bf16[4,128,512]{2,1,0:T(8,128)(2,1)S(1)} %all-to-all-done.2.sums_ref, bf16[256,128]{1,0:T(8,128)(2,1)S(1)} %copy-done.2, bf16[2,256,128]{2,1,0:T(8,128)(2,1)S(1)} %copy-done.1, bf16[2,2,256,128]{3,2,1,0:T(8,128)(2,1)S(1)} %collective-permute-done.3.d_ref, ...), custom_call_target="tpu_custom_call" | custom-call | tf_op jit(solution)/shard_map/pallas_call | solution.py:241
Async XLA Ops:
  9.6 49.6 %copy-start = (bf16[2,2,128,2048]{3,2,1,0:T(8,128)(2,1)S(1)}, bf16[2,2,128,2048]{3,2,1,0:T(8,128)(2,1)}, u32[]{:S(2)}) copy-start(bf16[2,2,128,2048]{3,2,1,0:T(8,128)(2,1)} %param.4) | copy-start | bytes 6291460
  10.9 28.0 %all-to-all-start = ((bf16[32,4,8,128]{3,2,1,0:T(8,128)(2,1)}), bf16[32,4,8,128]{3,2,1,0:T(8,128)(2,1)S(1)}, u32[]{:S(2)}, u32[]{:S(2)}) async-start(bf16[32,4,8,128]{3,2,1,0:T(8,128)(2,1)} %shard_map.53), calls=%async_computation | async-start | bytes 524288 | tf_op jit(solution)/shard_map/all_to_all | solution.py:296
  28.6 21.8 %collective-permute-start = (bf16[2,256,128]{2,1,0:T(8,128)(2,1)S(1)}, bf16[2,256,128]{2,1,0:T(8,128)(2,1)S(1)}, u32[]{:S(2)}, u32[]{:S(2)}) collective-permute-start(bf16[2,256,128]{2,1,0:T(8,128)(2,1)S(1)} %get-tuple-element.15.pair_ref), channel_id=1, source_target_pairs={{0,8},{4,12},{8,16},{12,20},{16,24},{20,28},{24,32},{28,36},{32,40... | collective-permute-start | bytes 393224 | tf_op jit(solution)/shard_map/ppermute | solution.py:269
  40.5 35.9 %all-to-all-start.1 = ((bf16[32,4,8,128]{3,2,1,0:T(8,128)(2,1)}), bf16[32,4,8,128]{3,2,1,0:T(8,128)(2,1)S(1)}, u32[]{:S(2)}, u32[]{:S(2)}) async-start(bf16[32,4,8,128]{3,2,1,0:T(8,128)(2,1)} %shard_map.54), calls=%async_computation.1 | async-start | bytes 524288 | tf_op jit(solution)/shard_map/all_to_all | solution.py:316
  51.2 16.8 %collective-permute-start.1 = (bf16[2,2,256,128]{3,2,1,0:T(8,128)(2,1)}, bf16[2,2,256,128]{3,2,1,0:T(8,128)(2,1)S(1)}, u32[]{:S(2)}, u32[]{:S(2)}) collective-permute-start(bf16[2,2,256,128]{3,2,1,0:T(8,128)(2,1)} %pad_maximum_fusion), channel_id=1, source_target_pairs={{0,4},{4,8},{8,12},{12,16},{16,20},{20,24},{24,28},{28,32},{32,36}... | collective-permute-start | bytes 786440 | tf_op jit(solution)/shard_map/ppermute | solution.py:269
  54.3 13.7 %collective-permute-start.2 = (bf16[2,256,128]{2,1,0:T(8,128)(2,1)S(1)}, bf16[2,256,128]{2,1,0:T(8,128)(2,1)}, u32[]{:S(2)}, u32[]{:S(2)}) collective-permute-start(bf16[2,256,128]{2,1,0:T(8,128)(2,1)S(1)} %collective-permute-done.a_ref), channel_id=1, source_target_pairs={{0,8},{4,12},{8,16},{12,20},{16,24},{20,28},{24,32},{28,36},{32,40... | collective-permute-start | bytes 393224 | tf_op jit(solution)/shard_map/ppermute | solution.py:269
  71.7 0.7 copy-start.3
  72.3 12.6 %copy-start.4 = (bf16[2,256,128]{2,1,0:T(8,128)(2,1)S(1)}, bf16[2,256,128]{2,1,0:T(8,128)(2,1)}, u32[]{:S(2)}) copy-start(bf16[2,256,128]{2,1,0:T(8,128)(2,1)} %copy-done.3) | copy-start | bytes 393220
  72.3 18.7 %collective-permute-start.3 = (bf16[2,2,256,128]{3,2,1,0:T(8,128)(2,1)}, bf16[2,2,256,128]{3,2,1,0:T(8,128)(2,1)S(1)}, u32[]{:S(2)}, u32[]{:S(2)}) collective-permute-start(bf16[2,2,256,128]{3,2,1,0:T(8,128)(2,1)} %get-tuple-element.21), channel_id=1, source_target_pairs={{4,0},{8,4},{12,8},{16,12},{20,16},{24,20},{28,24},{32,28},{36,32}... | collective-permute-start | bytes 786440 | tf_op jit(solution)/shard_map/ppermute | solution.py:269
  76.4 30.2 %copy-start.1 = (bf16[2,256,128]{2,1,0:T(8,128)(2,1)S(1)}, bf16[2,256,128]{2,1,0:T(8,128)(2,1)}, u32[]{:S(2)}) copy-start(bf16[2,256,128]{2,1,0:T(8,128)(2,1)} %get-tuple-element.20.mid_ref) | copy-start | bytes 393220
  76.4 30.2 %copy-start.2 = (bf16[256,128]{1,0:T(8,128)(2,1)S(1)}, bf16[256,128]{1,0:T(8,128)(2,1)}, u32[]{:S(2)}) copy-start(bf16[256,128]{1,0:T(8,128)(2,1)} %get-tuple-element.19.dq_ref) | copy-start | bytes 196612
  78.6 28.0 %all-to-all-start.2 = ((bf16[4,128,512]{2,1,0:T(8,128)(2,1)}), bf16[4,128,512]{2,1,0:T(8,128)(2,1)S(1)}, u32[]{:S(2)}, u32[]{:S(2)}) async-start(bf16[4,128,512]{2,1,0:T(8,128)(2,1)} %shard_map.55), calls=%async_computation.2 | async-start | bytes 1048576 | tf_op jit(solution)/shard_map/all_to_all | solution.py:330
  85.0 17.1 %collective-permute-start.4 = (bf16[2,256,128]{2,1,0:T(8,128)(2,1)S(1)}, bf16[2,256,128]{2,1,0:T(8,128)(2,1)S(1)}, u32[]{:S(2)}, u32[]{:S(2)}) collective-permute-start(bf16[2,256,128]{2,1,0:T(8,128)(2,1)S(1)} %copy-done.4), channel_id=1, source_target_pairs={{16,0},{20,4},{24,8},{28,12},{32,16},{36,20},{40,24},{44,28},{48,3... | collective-permute-start | bytes 393224 | tf_op jit(solution)/shard_map/ppermute | solution.py:269
  92.0 14.5 %collective-permute-start.5 = (bf16[2,256,128]{2,1,0:T(8,128)(2,1)S(1)}, bf16[2,256,128]{2,1,0:T(8,128)(2,1)S(1)}, u32[]{:S(2)}, u32[]{:S(2)}) collective-permute-start(bf16[2,256,128]{2,1,0:T(8,128)(2,1)S(1)} %shard_map.56), channel_id=1, source_target_pairs={{8,0},{12,4},{16,8},{20,12},{24,16},{28,20},{32,24},{36,28},{40,32... | collective-permute-start | bytes 393224 | tf_op jit(solution)/shard_map/ppermute | solution.py:269

commit v3 on v2

--- a/solution.py
+++ b/solution.py
@@ -120,7 +120,10 @@
         other.wait()
 
 
-def local_grad_kernel(heads, og_ref, w_ref, g_ref):
+def local_grad_kernel(heads, og_ref, w_ref, pair_ref, a_ref, g_ref, both_ref, sem):
+    load = pltpu.make_async_copy(pair_ref, both_ref.at[0], sem.at[0])
+    load.start()
+    both_ref[1] = a_ref[...]
     parts, tokens, width = og_ref.shape
     hd = g_ref.shape[1]
     g = sum(
@@ -130,6 +133,7 @@
     for h in range(heads):
         own = mm_nt(same, g[h * hd : (h + 1) * hd])
         g_ref[h * tokens : (h + 1) * tokens] = own.astype(BF16)
+    load.wait()
 
 
 def local_kernel(
@@ -287,7 +291,16 @@
     )
     a = shifted(pair, 2)
     og = lax.all_gather(out_grad, "head", axis=0)
-    both = jnp.stack([pair, a])
+    g_local, both = call(
+        kernel(local_grad_kernel, heads),
+        [(flat, BF16), ((2, *pair_of), BF16)],
+        og,
+        w,
+        pair,
+        a,
+        far=(2,),
+        scratch=(1,),
+    )
     b = shifted(both, 1)
     c = shifted(a, 2)
     (send,) = call(
@@ -295,7 +308,6 @@
     )
     got = lax.all_to_all(send, "line", 0, 0, tiled=True)
     flat, pair_of = (rows, hd), (2, rows, hd)
-    (g_local,) = call(kernel(local_grad_kernel, heads), [(flat, BF16)], og, w)
     away = (wide, flat, pair_of, pair_of)
     one_three, four, attended, local_dq, mid, two = call(
         kernel(local_kernel, heads, scale),

time: 108 us -> 119 us (1.10)
  the two profiles are of different devices: /device:TPU:55 before, /device:TPU:114 now
where the time goes in v3:
time: 119 us
  starting transfers between devices  47.7 us (40%)
  blocking collectives  36.2 us (30%)
  waiting for transfers between devices  21.6 us (18%)
  Pallas kernels  10.9 us (9%)
  local copies, waits for them, and re-layouts  1.58 us (1%)
    ppermute x6, starting transfers between devices, shifted(): return lax.ppermute(value, seq, pairs)  32.6 us
    all_to_all x1, blocking collectives, layer(): got = lax.all_to_all(send, 'line', 0, 0, tiled=True)  29.2 us
    ppermute x6, waiting for transfers between devices, shifted(): return lax.ppermute(value, seq, pairs)  21.6 us
    pallas_call x8, Pallas kernels, call(): pl.pallas_call(kernel, out_shape=made, in_specs=ins, out_specs=[hbm if n...  10.9 us
    all_to_all x1, starting transfers between devices, layer(): returned = lax.all_to_all(results, 'line', 0, 0, tiled=True)  10.1 us
    all_gather x1, blocking collectives, layer(): og = lax.all_gather(out_grad, 'head', axis=0)  6.98 us
    all_to_all x1, starting transfers between devices, layer(): sums = lax.all_to_all(partial, 'head', 0, 0, tiled=True)  5 us
  transfers between devices with their start and end apart: 8, of which 4 were waited for; matrix products, arithmetic and copies ran while one was open for 0% of the time, Pallas kernels for 5%

profile of v3, /device:TPU:114, one launch (start us, length us, event | category | flops | bytes accessed | tf_op | source)
XLA Modules:
  0.0 118.8 jit_solution(7444163559658639988)
XLA Ops:
  0.6 7.0 %all-gather = bf16[512,512]{1,0:T(8,128)(2,1)S(1)} all-gather(bf16[128,512]{1,0:T(8,128)(2,1)} %param.5), channel_id=2, replica_groups=mesh['line'=32,'quarter'=4,'head'=4] {'head'}, dimensions={0}, use_global_device_ids=true | all-gather | bytes 655360 | tf_op jit(solution)/shard_map/all_gather | solution.py:293
  7.6 1.4 %shard_map.50 = (bf16[2,256,128]{2,1,0:T(8,128)(2,1)S(1)}, bf16[256,128]{1,0:T(8,128)(2,1)S(1)}, bf16[4,256,512]{2,1,0:T(8,128)(2,1)S(1)}, bf16[3,256,128]{2,1,0:T(8,128)(2,1)S(1)}) custom-call(bf16[2,3,256,128]{3,2,1,0:T(8,128)(2,1)} %bitcast.10, bf16[512,2048]{1,0:T(8,128)(2,1)} %bitcast.5), custom_call_target="tpu_custom_call" | custom-call | tf_op jit(solution)/shard_map/pallas_call | solution.py:245
  9.1 0.0 copy-start.1
  9.1 0.0 copy-start
  9.1 0.7 shard_map.53
  9.8 29.2 %all_to_all.15.in_ref = bf16[32,4,8,128]{3,2,1,0:T(8,128)(2,1)S(1)} all-to-all(bf16[32,4,8,128]{3,2,1,0:T(8,128)(2,1)S(1)} %shard_map.53), channel_id=1, replica_groups=mesh['line'=32,'quarter'=4,'head'=4] {'line'}, dimensions={0} | all-to-all | bytes 524288 | tf_op jit(solution)/shard_map/all_to_all | solution.py:309
  38.9 1.6 %shard_map.54 = bf16[32,4,8,128]{3,2,1,0:T(8,128)(2,1)} custom-call(bf16[32,4,8,128]{3,2,1,0:T(8,128)(2,1)S(1)} %all_to_all.15.in_ref), custom_call_target="tpu_custom_call" | custom-call | tf_op jit(solution)/shard_map/pallas_call | solution.py:245
  40.5 10.1 %all-to-all-start.1 = ((bf16[32,4,8,128]{3,2,1,0:T(8,128)(2,1)}), bf16[32,4,8,128]{3,2,1,0:T(8,128)(2,1)S(1)}, u32[]{:S(2)}, u32[]{:S(2)}) async-start(bf16[32,4,8,128]{3,2,1,0:T(8,128)(2,1)} %shard_map.54), calls=%async_computation.1 | async-start | bytes 524288 | tf_op jit(solution)/shard_map/all_to_all | solution.py:328
  50.6 3.2 %collective-permute-start = (bf16[2,256,128]{2,1,0:T(8,128)(2,1)S(1)}, bf16[2,256,128]{2,1,0:T(8,128)(2,1)S(1)}, u32[]{:S(2)}, u32[]{:S(2)}) collective-permute-start(bf16[2,256,128]{2,1,0:T(8,128)(2,1)S(1)} %get-tuple-element.17.pair_ref), channel_id=1, source_target_pairs={{0,8},{4,12},{8,16},{12,20},{16,24},{20,28},{24,32},{28,36},{32,40... | collective-permute-start | bytes 393224 | tf_op jit(solution)/shard_map/ppermute | solution.py:273
  53.8 4.9 %collective-permute-done.a_ref = bf16[2,256,128]{2,1,0:T(8,128)(2,1)S(1)} collective-permute-done((bf16[2,256,128]{2,1,0:T(8,128)(2,1)S(1)}, bf16[2,256,128]{2,1,0:T(8,128)(2,1)S(1)}, u32[]{:S(2)}, u32[]{:S(2)}) %collective-permute-start) | collective-permute-done | bytes 131104 | tf_op jit(solution)/shard_map/ppermute | solution.py:273
  58.8 0.0 copy-done.1
  58.8 0.0 copy-done
  58.8 0.9 shard_map.51
  59.7 6.0 %collective-permute-start.1 = (bf16[2,2,256,128]{3,2,1,0:T(8,128)(2,1)S(1)}, bf16[2,2,256,128]{3,2,1,0:T(8,128)(2,1)S(1)}, u32[]{:S(2)}, u32[]{:S(2)}) collective-permute-start(bf16[2,2,256,128]{3,2,1,0:T(8,128)(2,1)S(1)} %get-tuple-element.19), channel_id=1, source_target_pairs={{0,4},{4,8},{8,12},{12,16},{16,20},{20,24},{24,28},{28,32},{32,36}... | collective-permute-start | bytes 786440 | tf_op jit(solution)/shard_map/ppermute | solution.py:273
  65.7 8.4 %collective-permute-start.2 = (bf16[2,256,128]{2,1,0:T(8,128)(2,1)S(1)}, bf16[2,256,128]{2,1,0:T(8,128)(2,1)S(1)}, u32[]{:S(2)}, u32[]{:S(2)}) collective-permute-start(bf16[2,256,128]{2,1,0:T(8,128)(2,1)S(1)} %collective-permute-done.a_ref), channel_id=1, source_target_pairs={{0,8},{4,12},{8,16},{12,20},{16,24},{20,28},{24,32},{28,36},{32,40... | collective-permute-start | bytes 393224 | tf_op jit(solution)/shard_map/ppermute | solution.py:273
  74.2 4.9 %collective-permute-done.2.c_ref = bf16[2,256,128]{2,1,0:T(8,128)(2,1)S(1)} collective-permute-done((bf16[2,256,128]{2,1,0:T(8,128)(2,1)S(1)}, bf16[2,256,128]{2,1,0:T(8,128)(2,1)S(1)}, u32[]{:S(2)}, u32[]{:S(2)}) %collective-permute-start.2) | collective-permute-done | bytes 131104 | tf_op jit(solution)/shard_map/ppermute | solution.py:273
  79.0 0.0 collective-permute-done.1.b_ref
  79.0 0.0 copy-start.2
  79.0 0.9 copy-done.2
  80.0 2.0 %shard_map.52 = (bf16[2,2,256,128]{3,2,1,0:T(8,128)(2,1)S(1)}, bf16[2,256,128]{2,1,0:T(8,128)(2,1)S(1)}, bf16[128,256]{1,0:T(8,128)(2,1)}, bf16[256,128]{1,0:T(8...) custom-call(s32[1]{0:T(128)} %bitcast.rank_ref, ...), custom_call_target="tpu_custom_call" | custom-call | tf_op jit(solution)/shard_map/pallas_call | solution.py:245
  82.0 0.0 copy-start.5
  82.0 0.6 copy-done.5
  82.7 0.0 copy-start.6
  82.7 2.0 %collective-permute-start.3 = (bf16[2,2,256,128]{3,2,1,0:T(8,128)(2,1)S(1)}, bf16[2,2,256,128]{3,2,1,0:T(8,128)(2,1)S(1)}, u32[]{:S(2)}, u32[]{:S(2)}) collective-permute-start(bf16[2,2,256,128]{3,2,1,0:T(8,128)(2,1)S(1)} %get-tuple-element.25), channel_id=1, source_target_pairs={{4,0},{8,4},{12,8},{16,12},{20,16},{24,20},{28,24},{32,28},{36,32}... | collective-permute-start | bytes 786440 | tf_op jit(solution)/shard_map/ppermute | solution.py:273
  84.7 0.0 all-to-all-done.1.back_ref
  84.7 0.0 copy-start.3
  84.7 0.0 copy-start.4
  84.7 2.1 %shard_map.55 = bf16[4,128,512]{2,1,0:T(8,128)(2,1)} custom-call(bf16[128,256]{1,0:T(8,128)(2,1)} %get-tuple-element.20.attended_ref, bf16[32,4,8,128]{3,2,1,0:T(8,128)(2,1)S(1)} %all-to-all-done.1.back_ref, bf16[512,2048]{1,0:T(8,128)(2,1)S(1)} %bitcast.7), custom_call_target="tpu_custom_call" | custom-call | tf_op jit(solution)/shard_map/pallas_call | solution.py:245
  86.9 5.0 %all-to-all-start.2 = ((bf16[4,128,512]{2,1,0:T(8,128)(2,1)}), bf16[4,128,512]{2,1,0:T(8,128)(2,1)S(1)}, u32[]{:S(2)}, u32[]{:S(2)}) async-start(bf16[4,128,512]{2,1,0:T(8,128)(2,1)} %shard_map.55), calls=%async_computation.2 | async-start | bytes 1048576 | tf_op jit(solution)/shard_map/all_to_all | solution.py:342
  91.9 0.0 copy-done.6
  91.9 11.1 %collective-permute-start.4 = (bf16[2,256,128]{2,1,0:T(8,128)(2,1)S(1)}, bf16[2,256,128]{2,1,0:T(8,128)(2,1)S(1)}, u32[]{:S(2)}, u32[]{:S(2)}) collective-permute-start(bf16[2,256,128]{2,1,0:T(8,128)(2,1)S(1)} %copy-done.6), channel_id=1, source_target_pairs={{16,0},{20,4},{24,8},{28,12},{32,16},{36,20},{40,24},{44,28},{48,3... | collective-permute-start | bytes 393224 | tf_op jit(solution)/shard_map/ppermute | solution.py:273
  103.0 0.0 collective-permute-done.3.d_ref
  103.0 0.9 shard_map.56
  103.9 1.9 %collective-permute-start.5 = (bf16[2,256,128]{2,1,0:T(8,128)(2,1)S(1)}, bf16[2,256,128]{2,1,0:T(8,128)(2,1)S(1)}, u32[]{:S(2)}, u32[]{:S(2)}) collective-permute-start(bf16[2,256,128]{2,1,0:T(8,128)(2,1)S(1)} %shard_map.56), channel_id=1, source_target_pairs={{8,0},{12,4},{16,8},{20,12},{24,16},{28,20},{32,24},{36,28},{40,32... | collective-permute-start | bytes 393224 | tf_op jit(solution)/shard_map/ppermute | solution.py:273
  105.9 2.1 %collective-permute-done.4.e_ref = bf16[2,256,128]{2,1,0:T(8,128)(2,1)S(1)} collective-permute-done((bf16[2,256,128]{2,1,0:T(8,128)(2,1)S(1)}, bf16[2,256,128]{2,1,0:T(8,128)(2,1)S(1)}, u32[]{:S(2)}, u32[]{:S(2)}) %collective-permute-start.4) | collective-permute-done | bytes 131104 | tf_op jit(solution)/shard_map/ppermute | solution.py:273
  108.0 9.6 %collective-permute-done.5.f_ref = bf16[2,256,128]{2,1,0:T(8,128)(2,1)S(1)} collective-permute-done((bf16[2,256,128]{2,1,0:T(8,128)(2,1)S(1)}, bf16[2,256,128]{2,1,0:T(8,128)(2,1)S(1)}, u32[]{:S(2)}, u32[]{:S(2)}) %collective-permute-start.5) | collective-permute-done | bytes 131104 | tf_op jit(solution)/shard_map/ppermute | solution.py:273
  117.6 0.0 all-to-all-done.2.sums_ref
  117.6 0.0 copy-done.3
  117.6 0.0 copy-done.4
  117.6 1.1 shard_map.57
Async XLA Ops:
  9.1 49.7 %copy-start.1 = (bf16[2,256,128]{2,1,0:T(8,128)(2,1)}, bf16[2,256,128]{2,1,0:T(8,128)(2,1)S(1)}, u32[]{:S(2)}) copy-start(bf16[2,256,128]{2,1,0:T(8,128)(2,1)S(1)} %get-tuple-element.17.pair_ref) | copy-start | bytes 393220
  9.1 49.7 %copy-start = (bf16[2,2,128,2048]{3,2,1,0:T(8,128)(2,1)S(1)}, bf16[2,2,128,2048]{3,2,1,0:T(8,128)(2,1)}, u32[]{:S(2)}) copy-start(bf16[2,2,128,2048]{3,2,1,0:T(8,128)(2,1)} %param.4) | copy-start | bytes 6291460
  40.5 44.2 %all-to-all-start.1 = ((bf16[32,4,8,128]{3,2,1,0:T(8,128)(2,1)}), bf16[32,4,8,128]{3,2,1,0:T(8,128)(2,1)S(1)}, u32[]{:S(2)}, u32[]{:S(2)}) async-start(bf16[32,4,8,128]{3,2,1,0:T(8,128)(2,1)} %shard_map.54), calls=%async_computation.1 | async-start | bytes 524288 | tf_op jit(solution)/shard_map/all_to_all | solution.py:328
  50.6 8.1 %collective-permute-start = (bf16[2,256,128]{2,1,0:T(8,128)(2,1)S(1)}, bf16[2,256,128]{2,1,0:T(8,128)(2,1)S(1)}, u32[]{:S(2)}, u32[]{:S(2)}) collective-permute-start(bf16[2,256,128]{2,1,0:T(8,128)(2,1)S(1)} %get-tuple-element.17.pair_ref), channel_id=1, source_target_pairs={{0,8},{4,12},{8,16},{12,20},{16,24},{20,28},{24,32},{28,36},{32,40... | collective-permute-start | bytes 393224 | tf_op jit(solution)/shard_map/ppermute | solution.py:273
  59.7 19.4 %collective-permute-start.1 = (bf16[2,2,256,128]{3,2,1,0:T(8,128)(2,1)S(1)}, bf16[2,2,256,128]{3,2,1,0:T(8,128)(2,1)S(1)}, u32[]{:S(2)}, u32[]{:S(2)}) collective-permute-start(bf16[2,2,256,128]{3,2,1,0:T(8,128)(2,1)S(1)} %get-tuple-element.19), channel_id=1, source_target_pairs={{0,4},{4,8},{8,12},{12,16},{16,20},{20,24},{24,28},{28,32},{32,36}... | collective-permute-start | bytes 786440 | tf_op jit(solution)/shard_map/ppermute | solution.py:273
  65.7 13.3 %collective-permute-start.2 = (bf16[2,256,128]{2,1,0:T(8,128)(2,1)S(1)}, bf16[2,256,128]{2,1,0:T(8,128)(2,1)S(1)}, u32[]{:S(2)}, u32[]{:S(2)}) collective-permute-start(bf16[2,256,128]{2,1,0:T(8,128)(2,1)S(1)} %collective-permute-done.a_ref), channel_id=1, source_target_pairs={{0,8},{4,12},{8,16},{12,20},{16,24},{20,28},{24,32},{28,36},{32,40... | collective-permute-start | bytes 393224 | tf_op jit(solution)/shard_map/ppermute | solution.py:273
  79.0 0.9 copy-start.2
  82.0 0.7 copy-start.5
  82.7 9.2 %copy-start.6 = (bf16[2,256,128]{2,1,0:T(8,128)(2,1)S(1)}, bf16[2,256,128]{2,1,0:T(8,128)(2,1)}, u32[]{:S(2)}) copy-start(bf16[2,256,128]{2,1,0:T(8,128)(2,1)} %copy-done.5) | copy-start | bytes 393220
  82.7 20.3 %collective-permute-start.3 = (bf16[2,2,256,128]{3,2,1,0:T(8,128)(2,1)S(1)}, bf16[2,2,256,128]{3,2,1,0:T(8,128)(2,1)S(1)}, u32[]{:S(2)}, u32[]{:S(2)}) collective-permute-start(bf16[2,2,256,128]{3,2,1,0:T(8,128)(2,1)S(1)} %get-tuple-element.25), channel_id=1, source_target_pairs={{4,0},{8,4},{12,8},{16,12},{20,16},{24,20},{28,24},{32,28},{36,32}... | collective-permute-start | bytes 786440 | tf_op jit(solution)/shard_map/ppermute | solution.py:273
  84.7 32.9 %copy-start.3 = (bf16[2,256,128]{2,1,0:T(8,128)(2,1)S(1)}, bf16[2,256,128]{2,1,0:T(8,128)(2,1)}, u32[]{:S(2)}) copy-start(bf16[2,256,128]{2,1,0:T(8,128)(2,1)} %get-tuple-element.24.mid_ref) | copy-start | bytes 393220
  84.7 32.9 %copy-start.4 = (bf16[256,128]{1,0:T(8,128)(2,1)S(1)}, bf16[256,128]{1,0:T(8,128)(2,1)}, u32[]{:S(2)}) copy-start(bf16[256,128]{1,0:T(8,128)(2,1)} %get-tuple-element.23.dq_ref) | copy-start | bytes 196612
  86.9 30.7 %all-to-all-start.2 = ((bf16[4,128,512]{2,1,0:T(8,128)(2,1)}), bf16[4,128,512]{2,1,0:T(8,128)(2,1)S(1)}, u32[]{:S(2)}, u32[]{:S(2)}) async-start(bf16[4,128,512]{2,1,0:T(8,128)(2,1)} %shard_map.55), calls=%async_computation.2 | async-start | bytes 1048576 | tf_op jit(solution)/shard_map/all_to_all | solution.py:342
  91.9 16.1 %collective-permute-start.4 = (bf16[2,256,128]{2,1,0:T(8,128)(2,1)S(1)}, bf16[2,256,128]{2,1,0:T(8,128)(2,1)S(1)}, u32[]{:S(2)}, u32[]{:S(2)}) collective-permute-start(bf16[2,256,128]{2,1,0:T(8,128)(2,1)S(1)} %copy-done.6), channel_id=1, source_target_pairs={{16,0},{20,4},{24,8},{28,12},{32,16},{36,20},{40,24},{44,28},{48,3... | collective-permute-start | bytes 393224 | tf_op jit(solution)/shard_map/ppermute | solution.py:273
  103.9 13.7 %collective-permute-start.5 = (bf16[2,256,128]{2,1,0:T(8,128)(2,1)S(1)}, bf16[2,256,128]{2,1,0:T(8,128)(2,1)S(1)}, u32[]{:S(2)}, u32[]{:S(2)}) collective-permute-start(bf16[2,256,128]{2,1,0:T(8,128)(2,1)S(1)} %shard_map.56), channel_id=1, source_target_pairs={{8,0},{12,4},{16,8},{20,12},{24,16},{28,20},{32,24},{36,28},{40,32... | collective-permute-start | bytes 393224 | tf_op jit(solution)/shard_map/ppermute | solution.py:273
